TPU v7x, 32 devices: a whole 2x2x4 slice. The times are simulated.
32 devices in a mesh: video: 2 (over y), row: 4 (over z), col: 2 (over x), sub: 2 (over core).
Axes of the slice: x: 2, y: 2, z: 4, core: 2. Of those that a mesh axis runs over, the one named last changes fastest.
Arguments:
- mid_latent: bfloat16 [4, 8, 160, 256], P('video', ('row', 'col')), parts along dimension 0, may hold values from -6 to 6
- mid_cache: bfloat16 [4, 8, 160, 256], P('video', ('row', 'col')), parts along dimension 0, may hold values from -6 to 6
- mid_kernel: bfloat16 [3, 3, 3, 256, 256], P(None, None, None, None, 'sub'), may hold values from -0.078125 to 0.078125
- mid_offset: float32 [256], P('sub'), may hold values from -3 to 3
- fine_cache: bfloat16 [4, 16, 320, 256], P('video', 'row', 'col'), parts along dimension 0, may hold values from -6 to 6
- fine_kernel: bfloat16 [3, 3, 3, 256, 256], P(None, None, None, None, 'sub'), may hold values from -0.078125 to 0.078125
- fine_offset: float32 [256], P('sub'), may hold values from -3 to 3
Outputs:
- decoded: bfloat16 [4, 16, 320, 256], P('video', 'row', 'col', 'sub'), parts along dimension 0
There are 2 independent parts, one for each index of `video`. A program takes and returns all parts, laid end to end along the dimension named above; an argument that names none is the same for every part. Nothing has to cross between parts.
All inputs are finite; a program needn't handle non-finite values.
Results may differ from a plain program's by a relative error of at most 0.0045.
Values may be sent and summed in bfloat16 or wider, within the bound.
No kernel may reach another device: no remote copies, remote signals or barrier semaphores. Data moves between devices by JAX's collectives and lax.ppermute only.
A program may use at most 64 MiB of HBM per device.

v0:
```python
import jax
import jax.numpy as jnp
from jax import lax
from jax.sharding import PartitionSpec as P


def with_halo(x, sides, width):
    for axis, dim in sides:
        count, length = (lax.axis_size(axis), x.shape[dim])
        up = [(i, (i + 1) % count) for i in range(count - 1)]
        down = [(j, i) for i, j in up]
        last = lax.slice_in_dim(x, length - width, length, axis=dim)
        initial = lax.slice_in_dim(x, 0, width, axis=dim)
        before = lax.ppermute(last, axis, up)
        after = lax.ppermute(initial, axis, down)
        x = jnp.concatenate([before, x, after], axis=dim)
    return x


def conv_valid(frames, kernel, offset):
    result = lax.conv_general_dilated(
        frames[None],
        kernel,
        (1, 1, 1),
        "VALID",
        dimension_numbers=("NDHWC", "DHWIO", "NDHWC"),
        preferred_element_type=jnp.float32,
    )
    return (result[0] + offset).astype(jnp.bfloat16)


def double_size(field):
    return jnp.repeat(jnp.repeat(field, 2, axis=1), 2, axis=2)


def body(mid_latent, mid_cache, mid_kernel, mid_offset, fine_cache, fine_kernel, fine_offset):
    mid_frames = jnp.concatenate([mid_cache, mid_latent], axis=0)
    padded = with_halo(mid_frames, ((("row", "col"), 1),), 1)
    padded = jnp.pad(padded, ((0, 0), (0, 0), (1, 1), (0, 0)))
    strip_out = conv_valid(padded, mid_kernel, mid_offset)
    mid_out = lax.all_to_all(strip_out, "col", split_axis=2, concat_axis=1, tiled=True)
    gathered = lax.all_gather(mid_out, "sub", axis=3, tiled=True)
    activated = jax.nn.silu(gathered.astype(jnp.float32)).astype(jnp.bfloat16)
    upsampled = double_size(activated)
    fine_frames = with_halo(
        jnp.concatenate([fine_cache, upsampled], axis=0), (("row", 1), ("col", 2)), 1
    )
    return conv_valid(fine_frames, fine_kernel, fine_offset)


def solution(mesh):
    placed = (
        P("video", ("row", "col"), None, None),
        P("video", ("row", "col"), None, None),
        P(None, None, None, None, "sub"),
        P("sub"),
        P("video", "row", "col", None),
        P(None, None, None, None, "sub"),
        P("sub"),
    )
    return jax.shard_map(
        body, mesh=mesh, in_specs=placed, out_specs=P("video", "row", "col", "sub"), check_vma=False
    )
```

profile of v0, /device:TPU:0, one launch (start us, length us, event | category | flops | bytes accessed | tf_op | source)
XLA Modules:
  0.0 73.7 jit_solution(11497965046768141377)
XLA Ops:
  0.0 0.0 copy-start
  0.0 1.1 %constant_dynamic-update-slice_fusion.1 = bf16[4,1,160,256]{3,2,1,0:T(8,128)(2,1)S(1)} fusion(bf16[2,1,160,256]{3,2,1,0:T(8,128)(2,1)} %param.8), kind=kLoop, calls=%fused_computation.45 | loop fusion | bytes 327680
  1.1 0.9 %constant_dynamic-update-slice_fusion = bf16[4,1,160,256]{3,2,1,0:T(8,128)(2,1)S(1)} fusion(bf16[4,1,160,256]{3,2,1,0:T(8,128)(2,1)S(1)} %constant_dynamic-update-slice_fusion.1, bf16[2,1,160,256]{3,2,1,0:T(8,128)(2,1)} %param.7), kind=kLoop, calls=%fused_computation.44 | loop fusion | bytes 327680 | tf_op jit(solution)/shard_map/concatenate | solution.py:37
  2.0 1.3 %collective-permute-start.1 = (bf16[4,1,160,256]{3,2,1,0:T(8,128)(2,1)S(1)}, bf16[4,1,160,256]{3,2,1,0:T(8,128)(2,1)S(1)}, u32[]{:S(2)}, u32[]{:S(2)}) collective-permute-start(bf16[4,1,160,256]{3,2,1,0:T(8,128)(2,1)S(1)} %constant_dynamic-update-slice_fusion), channel_id=1, source_target_pairs={{2,0},{4,2},{6,4},{8,6},{10,8},{12,10},{14,12},{3,1},{5,3},{7,5},{... | collective-permute-start | bytes 983048 | tf_op jit(solution)/shard_map/ppermute | solution.py:15
  3.3 5.5 %collective-permute-start = (bf16[4,1,160,256]{3,2,1,0:T(8,128)(2,1)S(1)}, bf16[4,1,160,256]{3,2,1,0:T(8,128)(2,1)S(1)}, u32[]{:S(2)}, u32[]{:S(2)}) collective-permute-start(bf16[4,1,160,256]{3,2,1,0:T(8,128)(2,1)S(1)} %constant_dynamic-update-slice_fusion), channel_id=1, source_target_pairs={{0,2},{2,4},{4,6},{6,8},{8,10},{10,12},{12,14},{1,3},{3,5},{5,7},{... | collective-permute-start | bytes 983048 | tf_op jit(solution)/shard_map/ppermute | solution.py:14
  8.8 5.8 %collective-permute-done.1 = bf16[4,1,160,256]{3,2,1,0:T(8,128)(2,1)S(1)} collective-permute-done((bf16[4,1,160,256]{3,2,1,0:T(8,128)(2,1)S(1)}, bf16[4,1,160,256]{3,2,1,0:T(8,128)(2,1)S(1)}, u32[]{:S(2)}, u32[]{:S(2)}) %collective-permute-start.1) | collective-permute-done | bytes 327712 | tf_op jit(solution)/shard_map/ppermute | solution.py:15
  14.6 7.2 %collective-permute-done = bf16[4,1,160,256]{3,2,1,0:T(8,128)(2,1)S(1)} collective-permute-done((bf16[4,1,160,256]{3,2,1,0:T(8,128)(2,1)S(1)}, bf16[4,1,160,256]{3,2,1,0:T(8,128)(2,1)S(1)}, u32[]{:S(2)}, u32[]{:S(2)}) %collective-permute-start) | collective-permute-done | bytes 327712 | tf_op jit(solution)/shard_map/ppermute | solution.py:14
  21.7 0.3 fusion.25
  22.0 0.4 copy.42
  22.4 0.0 copy-start.3
  22.4 0.0 copy-start.4
  22.5 0.4 pad.5.clone
  22.9 0.1 copy.31
  23.0 0.9 %copy-done.3 = bf16[3,3,3,256,128]{4,3,2,1,0:T(8,128)(2,1)S(1)} copy-done((bf16[3,3,3,256,128]{4,3,2,1,0:T(8,128)(2,1)S(1)}, bf16[3,3,3,256,128]{4,3,2,1,0:T(8,128)(2,1)}, u32[]{:S(2)}) %copy-start.3) | copy-done | bytes 1769496
  23.9 0.0 copy-done.4
  23.9 0.0 copy-start.2
  23.9 1.4 %convolution_select_fusion = f32[2,1,8,21,128]{4,2,3,1,0:T(8,128)S(1)} fusion(bf16[3,3,3,256,128]{4,3,2,1,0:T(8,128)(2,1)S(1)} %copy-done.3, bf16[4,3,1,7,2,256]{5,3,4,1,0,2:T(8,128)(2,1)S(1)} %slice.20, bf16[4,3,1,8,21,256]{5,3,4,1,0,2:T(8,128)(2,1)S(1)} %copy.31, pred[8,21]{0,1:T(8,128)(4,1)S(1)} %copy-done.4), kind=kOutput, calls=%fused_computation.18 | convolution fusion | flops 597977088 | bytes 3059880 | tf_op jit(solution)/shard_map/conv_general_dilated | solution.py:21
  25.3 0.1 copy.32
  25.4 0.0 copy-done.2
  25.5 0.7 copy.34
  26.2 3.8 %all-to-all-start = ((bf16[2,1,160,128]{3,0,1,2:T(2,128)(2,1)}), bf16[2,1,160,128]{3,0,1,2:T(2,128)(2,1)S(1)}, u32[]{:S(2)}, u32[]{:S(2)}) async-start(bf16[2,1,160,128]{3,0,1,2:T(2,128)(2,1)} %copy.34), calls=%async_computation | async-start | bytes 163840 | tf_op jit(solution)/shard_map/all_to_all | solution.py:41
  29.9 1.1 %constant_dynamic-update-slice_fusion.3 = bf16[4,4,160,256]{3,2,1,0:T(8,128)(2,1)S(1)} fusion(bf16[2,4,160,256]{3,2,1,0:T(8,128)(2,1)} %param.11), kind=kLoop, calls=%fused_computation.47 | loop fusion | bytes 1310720
  31.1 3.1 %all-to-all-done = bf16[2,1,160,128]{3,0,1,2:T(2,128)(2,1)S(1)} async-done(((bf16[2,1,160,128]{3,0,1,2:T(2,128)(2,1)}), bf16[2,1,160,128]{3,0,1,2:T(2,128)(2,1)S(1)}, u32[]{:S(2)}, u32[]{:S(2)}) %all-to-all-start) | async-done | bytes 81952 | tf_op jit(solution)/shard_map/all_to_all | solution.py:41
  34.2 2.0 %all_gather.3 = bf16[2,2,80,256]{3,2,1,0:T(8,128)(2,1)S(1)} all-gather(bf16[2,2,80,128]{3,2,1,0:T(8,128)(2,1)S(1)} %bitcast.37), channel_id=1, replica_groups=mesh['video'=2,'row'=4,'col'=2,'sub'=2] {'sub'}, dimensions={3}, use_global_device_ids=true | all-gather | bytes 245760 | tf_op jit(solution)/shard_map/all_gather | solution.py:42
  36.1 0.1 fusion.32
  36.3 1.3 %broadcast_in_dim.16 = bf16[2,4,80,2,256]{4,3,2,1,0:T(2,128)(2,1)} broadcast(bf16[2,4,80,256]{3,2,1,0:T(8,128)(2,1)S(1)} %bitcast.35), dimensions={0,1,2,4} | broadcast | bytes 983040 | tf_op jit(solution)/shard_map/broadcast_in_dim | solution.py:33
  37.5 2.7 %reshape.30 = bf16[2,4,160,256]{3,2,1,0:T(8,128)(2,1)} reshape(bf16[2,4,80,2,256]{4,3,2,1,0:T(2,128)(2,1)} %broadcast_in_dim.16) | data formatting | bytes 1310720 | tf_op jit(solution)/shard_map/reshape | solution.py:33
  40.3 1.1 %constant_dynamic-update-slice_fusion.2 = bf16[4,4,160,256]{3,2,1,0:T(8,128)(2,1)S(1)} fusion(bf16[4,4,160,256]{3,2,1,0:T(8,128)(2,1)S(1)} %constant_dynamic-update-slice_fusion.3, bf16[2,4,160,256]{3,2,1,0:T(8,128)(2,1)} %reshape.30), kind=kLoop, calls=%fused_computation.46 | loop fusion | bytes 1310720 | tf_op jit(solution)/shard_map/concatenate | solution.py:46
  41.4 3.5 %collective-permute-start.2 = (bf16[4,1,160,256]{3,2,1,0:T(8,128)(2,1)S(1)}, bf16[4,1,160,256]{3,2,1,0:T(8,128)(2,1)S(1)}, u32[]{:S(2)}, u32[]{:S(2)}) collective-permute-start(bf16[4,1,160,256]{3,2,1,0:T(8,128)(2,1)S(1)} %get-tuple-element.7), channel_id=1, source_target_pairs={{0,4},{4,8},{8,12},{1,5},{5,9},{9,13},{2,6},{6,10},{10,14},{3,7},{... | collective-permute-start | bytes 983048 | tf_op jit(solution)/shard_map/ppermute | solution.py:14
  45.0 1.3 %collective-permute-start.3 = (bf16[4,1,160,256]{3,2,1,0:T(8,128)(2,1)S(1)}, bf16[4,1,160,256]{3,2,1,0:T(8,128)(2,1)S(1)}, u32[]{:S(2)}, u32[]{:S(2)}) collective-permute-start(bf16[4,1,160,256]{3,2,1,0:T(8,128)(2,1)S(1)} %get-tuple-element.8), channel_id=1, source_target_pairs={{4,0},{8,4},{12,8},{5,1},{9,5},{13,9},{6,2},{10,6},{14,10},{7,3},{... | collective-permute-start | bytes 983048 | tf_op jit(solution)/shard_map/ppermute | solution.py:15
  46.3 5.9 %collective-permute-done.2 = bf16[4,1,160,256]{3,2,1,0:T(8,128)(2,1)S(1)} collective-permute-done((bf16[4,1,160,256]{3,2,1,0:T(8,128)(2,1)S(1)}, bf16[4,1,160,256]{3,2,1,0:T(8,128)(2,1)S(1)}, u32[]{:S(2)}, u32[]{:S(2)}) %collective-permute-start.2) | collective-permute-done | bytes 327712 | tf_op jit(solution)/shard_map/ppermute | solution.py:14
  52.2 4.1 %collective-permute-done.3 = bf16[4,1,160,256]{3,2,1,0:T(8,128)(2,1)S(1)} collective-permute-done((bf16[4,1,160,256]{3,2,1,0:T(8,128)(2,1)S(1)}, bf16[4,1,160,256]{3,2,1,0:T(8,128)(2,1)S(1)}, u32[]{:S(2)}, u32[]{:S(2)}) %collective-permute-start.3) | collective-permute-done | bytes 327712 | tf_op jit(solution)/shard_map/ppermute | solution.py:15
  56.4 1.9 %collective-permute-start.4 = (bf16[4,6,1,256]{3,2,1,0:T(2,128)(2,1)S(1)}, bf16[4,6,1,256]{3,2,1,0:T(2,128)(2,1)S(1)}, u32[]{:S(2)}, u32[]{:S(2)}) collective-permute-start(bf16[4,6,1,256]{3,2,1,0:T(2,128)(2,1)S(1)} %get-tuple-element.5), channel_id=1, source_target_pairs={{0,2},{1,3},{4,6},{5,7},{8,10},{9,11},{12,14},{13,15},{16,18},{17,... | collective-permute-start | bytes 36872 | tf_op jit(solution)/shard_map/ppermute | solution.py:14
  58.3 1.5 %collective-permute-start.5 = (bf16[4,6,1,256]{3,2,1,0:T(2,128)(2,1)S(1)}, bf16[4,6,1,256]{3,2,1,0:T(2,128)(2,1)S(1)}, u32[]{:S(2)}, u32[]{:S(2)}) collective-permute-start(bf16[4,6,1,256]{3,2,1,0:T(2,128)(2,1)S(1)} %get-tuple-element.6), channel_id=1, source_target_pairs={{2,0},{3,1},{6,4},{7,5},{10,8},{11,9},{14,12},{15,13},{18,16},{19,... | collective-permute-start | bytes 36872 | tf_op jit(solution)/shard_map/ppermute | solution.py:15
  59.8 0.0 collective-permute-done.4
  59.8 4.2 %collective-permute-done.5 = bf16[4,6,1,256]{3,2,1,0:T(2,128)(2,1)S(1)} collective-permute-done((bf16[4,6,1,256]{3,2,1,0:T(2,128)(2,1)S(1)}, bf16[4,6,1,256]{3,2,1,0:T(2,128)(2,1)S(1)}, u32[]{:S(2)}, u32[]{:S(2)}) %collective-permute-start.5) | collective-permute-done | bytes 12320 | tf_op jit(solution)/shard_map/ppermute | solution.py:15
  64.0 1.3 %maximum_bitcast_fusion = bf16[4,6,1,162,256]{4,3,1,0,2:T(8,128)(2,1)S(1)} fusion(bf16[4,6,1,256]{3,2,1,0:T(2,128)(2,1)S(1)} %collective-permute-done.5, bf16[4,1,160,256]{3,2,1,0:T(8,128)(2,1)S(1)} %collective-permute-done.3, bf16[4,4,160,256]{3,2,1,0:T(8,128)(2,1)S(1)} %constant_dynamic-update-slice_fusion.2, ...), kind=kLoop, calls=%fused_computation.12 | loop fusion | flops 9953280 | bytes 3981312 | tf_op jit(solution)/shard_map/broadcast_in_dim | solution.py:22
  65.3 1.0 %copy.43 = bf16[4,6,1,162,256]{4,0,3,1,2:T(4,128)(2,1)S(1)} copy(bf16[4,6,1,162,256]{4,3,1,0,2:T(8,128)(2,1)S(1)} %maximum_bitcast_fusion) | data formatting | bytes 3981312
  66.4 0.8 %pad.7.clone = bf16[4,6,1,168,256]{4,0,3,1,2:T(4,128)(2,1)S(1)} pad(bf16[4,6,1,162,256]{4,0,3,1,2:T(4,128)(2,1)S(1)} %copy.43, bf16[]{:T(256)} %constant.4.clone.1), padding=0_0x0_0x0_0x0_6x0_0 | pad | bytes 4055042 | tf_op jit(solution)/shard_map/broadcast_in_dim | solution.py:22
  67.1 0.3 copy.38
  67.5 0.0 copy-done
  67.5 0.0 copy-start.1
  67.5 5.1 %fusion.10 = f32[2,4,8,21,128]{4,2,3,1,0:T(8,128)S(1)} fusion(bf16[3,3,3,256,128]{4,3,2,1,0:T(8,128)(2,1)S(1)} %copy-done, bf16[4,6,1,7,2,256]{5,3,4,1,0,2:T(8,128)(2,1)S(1)} %slice.24, bf16[4,6,1,8,21,256]{5,3,4,1,0,2:T(8,128)(2,1)S(1)} %copy.38, pred[8,21]{0,1:T(8,128)(4,1)S(1)} %copy-done.4), kind=kOutput, calls=%fused_computation.14 | convolution fusion | flops 2385125376 | bytes 4694184 | tf_op jit(solution)/shard_map/conv_general_dilated | solution.py:21
  72.6 0.2 copy.39
  72.8 0.0 copy-done.1
  72.8 0.1 fusion.27
  73.0 0.8 %copy.40 = bf16[2,4,160,128]{3,2,1,0:T(8,128)(2,1)} copy(bf16[2,4,160,128]{3,1,2,0:T(4,128)(2,1)S(1)} %fusion.27) | data formatting | bytes 655360 | tf_op jit(solution)/shard_map/convert_element_type | solution.py:29
  (8 shorter events, 0.2 us)
Async XLA Ops:
  0.0 67.5 %copy-start = (bf16[3,3,3,256,128]{4,3,2,1,0:T(8,128)(2,1)S(1)}, bf16[3,3,3,256,128]{4,3,2,1,0:T(8,128)(2,1)}, u32[]{:S(2)}) copy-start(bf16[3,3,3,256,128]{4,3,2,1,0:T(8,128)(2,1)} %param.12) | copy-start | bytes 5308420
  2.0 12.6 %collective-permute-start.1 = (bf16[4,1,160,256]{3,2,1,0:T(8,128)(2,1)S(1)}, bf16[4,1,160,256]{3,2,1,0:T(8,128)(2,1)S(1)}, u32[]{:S(2)}, u32[]{:S(2)}) collective-permute-start(bf16[4,1,160,256]{3,2,1,0:T(8,128)(2,1)S(1)} %constant_dynamic-update-slice_fusion), channel_id=1, source_target_pairs={{2,0},{4,2},{6,4},{8,6},{10,8},{12,10},{14,12},{3,1},{5,3},{7,5},{... | collective-permute-start | bytes 983048 | tf_op jit(solution)/shard_map/ppermute | solution.py:15
  3.3 18.5 %collective-permute-start = (bf16[4,1,160,256]{3,2,1,0:T(8,128)(2,1)S(1)}, bf16[4,1,160,256]{3,2,1,0:T(8,128)(2,1)S(1)}, u32[]{:S(2)}, u32[]{:S(2)}) collective-permute-start(bf16[4,1,160,256]{3,2,1,0:T(8,128)(2,1)S(1)} %constant_dynamic-update-slice_fusion), channel_id=1, source_target_pairs={{0,2},{2,4},{4,6},{6,8},{8,10},{10,12},{12,14},{1,3},{3,5},{5,7},{... | collective-permute-start | bytes 983048 | tf_op jit(solution)/shard_map/ppermute | solution.py:14
  22.4 1.5 %copy-start.3 = (bf16[3,3,3,256,128]{4,3,2,1,0:T(8,128)(2,1)S(1)}, bf16[3,3,3,256,128]{4,3,2,1,0:T(8,128)(2,1)}, u32[]{:S(2)}) copy-start(bf16[3,3,3,256,128]{4,3,2,1,0:T(8,128)(2,1)} %param.9) | copy-start | bytes 5308420
  22.4 1.5 %copy-start.4 = (pred[8,21]{0,1:T(8,128)(4,1)S(1)}, pred[8,21]{0,1:T(8,128)(4,1)}, u32[]{:S(2)}) copy-start(pred[8,21]{0,1:T(8,128)(4,1)} %constant.18) | copy-start | bytes 508
  23.9 1.5 %copy-start.2 = (f32[128]{0:T(128)S(1)}, f32[128]{0:T(128)}, u32[]{:S(2)}) copy-start(f32[128]{0:T(128)} %param.10) | copy-start | bytes 1540
  26.2 8.0 %all-to-all-start = ((bf16[2,1,160,128]{3,0,1,2:T(2,128)(2,1)}), bf16[2,1,160,128]{3,0,1,2:T(2,128)(2,1)S(1)}, u32[]{:S(2)}, u32[]{:S(2)}) async-start(bf16[2,1,160,128]{3,0,1,2:T(2,128)(2,1)} %copy.34), calls=%async_computation | async-start | bytes 163840 | tf_op jit(solution)/shard_map/all_to_all | solution.py:41
  41.4 10.8 %collective-permute-start.2 = (bf16[4,1,160,256]{3,2,1,0:T(8,128)(2,1)S(1)}, bf16[4,1,160,256]{3,2,1,0:T(8,128)(2,1)S(1)}, u32[]{:S(2)}, u32[]{:S(2)}) collective-permute-start(bf16[4,1,160,256]{3,2,1,0:T(8,128)(2,1)S(1)} %get-tuple-element.7), channel_id=1, source_target_pairs={{0,4},{4,8},{8,12},{1,5},{5,9},{9,13},{2,6},{6,10},{10,14},{3,7},{... | collective-permute-start | bytes 983048 | tf_op jit(solution)/shard_map/ppermute | solution.py:14
  45.0 11.4 %collective-permute-start.3 = (bf16[4,1,160,256]{3,2,1,0:T(8,128)(2,1)S(1)}, bf16[4,1,160,256]{3,2,1,0:T(8,128)(2,1)S(1)}, u32[]{:S(2)}, u32[]{:S(2)}) collective-permute-start(bf16[4,1,160,256]{3,2,1,0:T(8,128)(2,1)S(1)} %get-tuple-element.8), channel_id=1, source_target_pairs={{4,0},{8,4},{12,8},{5,1},{9,5},{13,9},{6,2},{10,6},{14,10},{7,3},{... | collective-permute-start | bytes 983048 | tf_op jit(solution)/shard_map/ppermute | solution.py:15
  56.4 3.4 %collective-permute-start.4 = (bf16[4,6,1,256]{3,2,1,0:T(2,128)(2,1)S(1)}, bf16[4,6,1,256]{3,2,1,0:T(2,128)(2,1)S(1)}, u32[]{:S(2)}, u32[]{:S(2)}) collective-permute-start(bf16[4,6,1,256]{3,2,1,0:T(2,128)(2,1)S(1)} %get-tuple-element.5), channel_id=1, source_target_pairs={{0,2},{1,3},{4,6},{5,7},{8,10},{9,11},{12,14},{13,15},{16,18},{17,... | collective-permute-start | bytes 36872 | tf_op jit(solution)/shard_map/ppermute | solution.py:14
  58.3 5.7 %collective-permute-start.5 = (bf16[4,6,1,256]{3,2,1,0:T(2,128)(2,1)S(1)}, bf16[4,6,1,256]{3,2,1,0:T(2,128)(2,1)S(1)}, u32[]{:S(2)}, u32[]{:S(2)}) collective-permute-start(bf16[4,6,1,256]{3,2,1,0:T(2,128)(2,1)S(1)} %get-tuple-element.6), channel_id=1, source_target_pairs={{2,0},{3,1},{6,4},{7,5},{10,8},{11,9},{14,12},{15,13},{18,16},{19,... | collective-permute-start | bytes 36872 | tf_op jit(solution)/shard_map/ppermute | solution.py:15
  67.5 5.3 %copy-start.1 = (f32[128]{0:T(128)S(1)}, f32[128]{0:T(128)}, u32[]{:S(2)}) copy-start(f32[128]{0:T(128)} %param.13) | copy-start | bytes 1540
where the time goes:
time: 74.2 us; the launch traced here: 73.7 us
  waiting for transfers between devices  30.3 us (41%)
  starting transfers between devices  18.7 us (25%)
  local copies, waits for them, and re-layouts  14 us (19%)
  matrix products  6.53 us (9%)
  blocking collectives  1.95 us (3%)
  other arithmetic  1.89 us (3%)
    ppermute x3, waiting for transfers between devices, with_halo(): after = lax.ppermute(initial, axis, down)  14.1 us
    ppermute x3, waiting for transfers between devices, with_halo(): before = lax.ppermute(last, axis, up)  13.1 us
    ppermute x3, starting transfers between devices, with_halo(): before = lax.ppermute(last, axis, up)  10.9 us
    conv_general_dilated x2, matrix products, conv_valid(): lax.conv_general_dilated(frames[None], kernel, (1, 1, 1), 'VALID', dimens...  6.53 us
    unnamed x14, local copies, waits for them, and re-layouts  4.5 us
    ppermute x3, starting transfers between devices, with_halo(): after = lax.ppermute(initial, axis, down)  4.06 us
    all_to_all x1, starting transfers between devices, body(): lax.all_to_all(strip_out, 'col', split_axis=2, concat_axis=1, tiled=True)  3.76 us
    all_to_all x1, waiting for transfers between devices, body(): lax.all_to_all(strip_out, 'col', split_axis=2, concat_axis=1, tiled=True)  3.1 us
  transfers between devices with their start and end apart: 7, of which 6 were waited for; matrix products, arithmetic and copies ran while one was open for 2% of the time, Pallas kernels for 0%

commit v1 on v0

--- a/solution.py
+++ b/solution.py
@@ -1,7 +1,15 @@
+import functools
+
 import jax
 import jax.numpy as jnp
 from jax import lax
+from jax.experimental import pallas as pl
+from jax.experimental.pallas import tpu as pltpu
 from jax.sharding import PartitionSpec as P
+
+BF16 = jnp.bfloat16
+F32 = jnp.float32
+PX = 16
 
 
 def with_halo(x, sides, width):
@@ -33,7 +41,7 @@
     return jnp.repeat(jnp.repeat(field, 2, axis=1), 2, axis=2)
 
 
-def body(mid_latent, mid_cache, mid_kernel, mid_offset, fine_cache, fine_kernel, fine_offset):
+def general_body(mid_latent, mid_cache, mid_kernel, mid_offset, fine_cache, fine_kernel, fine_offset):
     mid_frames = jnp.concatenate([mid_cache, mid_latent], axis=0)
     padded = with_halo(mid_frames, ((("row", "col"), 1),), 1)
     padded = jnp.pad(padded, ((0, 0), (0, 0), (1, 1), (0, 0)))
@@ -48,6 +56,332 @@
     return conv_valid(fine_frames, fine_kernel, fine_offset)
 
 
+def call(body, outs, args, scratch=(), flops=0, name=None):
+    vmem = pl.BlockSpec(memory_space=pltpu.VMEM)
+    many = isinstance(outs, (tuple, list))
+    listed = tuple(outs) if many else (outs,)
+    size = sum(a.size * a.dtype.itemsize for a in args) + sum(
+        o.size * o.dtype.itemsize for o in listed
+    )
+    return pl.pallas_call(
+        body,
+        out_shape=listed if many else outs,
+        in_specs=[vmem] * len(args),
+        out_specs=(vmem,) * len(listed) if many else vmem,
+        scratch_shapes=list(scratch),
+        cost_estimate=pl.CostEstimate(flops=flops, bytes_accessed=size, transcendentals=0),
+        name=name,
+    )(*args)
+
+
+def places():
+    return (
+        lax.axis_index("row"),
+        lax.axis_index("col"),
+        lax.axis_index("sub"),
+        lax.axis_size("row"),
+    )
+
+
+def shifted_sum(a, n):
+    rows = a.shape[0]
+    return (
+        pltpu.roll(a[:, n : n + 128], 1, 0)
+        + a[:, n + 128 : n + 256]
+        + pltpu.roll(a[:, n + 256 : n + 384], rows - 1, 0)
+    )
+
+
+def edged_sum(a):
+    rows = a.shape[0]
+    at = lax.broadcasted_iota(jnp.int32, (rows, 128), 0)
+    left = jnp.where(at == 0, 0.0, pltpu.roll(a[:, :128], 1, 0))
+    right = jnp.where(at == rows - 1, 0.0, pltpu.roll(a[:, 256:384], rows - 1, 0))
+    return left + a[:, 128:256] + right
+
+
+def lanes(parts):
+    return jnp.concatenate(parts, axis=1)
+
+
+def stacked(parts):
+    return jnp.concatenate(parts, axis=0)
+
+
+def dot(a, b):
+    return jnp.dot(a, b, preferred_element_type=F32)
+
+
+def pack_body(strip, cache, latent, fine, own, slant, side, edge):
+    _, c, s, _ = places()
+    width = cache.shape[2]
+    last = fine.shape[1] - 1
+    here = pl.multiple_of(c * (width - strip), 8)
+    there = pl.multiple_of((1 - c) * (width - strip), 8)
+    near = pl.multiple_of((1 - c) * (fine.shape[2] - PX), 16)
+    row = s * last
+    for f in range(2):
+        own[f] = cache[f, 0, pl.ds(here, strip), :]
+        own[2 + f] = latent[f, 0, pl.ds(here, strip), :]
+        slant[f * strip : (f + 1) * strip] = cache[f, 0, pl.ds(there, strip), :]
+        slant[(2 + f) * strip : (3 + f) * strip] = latent[f, 0, pl.ds(there, strip), :]
+        slant[4 * strip + PX * f : 4 * strip + PX * (f + 1)] = fine[f, row, pl.ds(near, PX), :]
+        edge[f] = fine[f, row]
+
+    @pl.when(s == 0)
+    def _():
+        for f in range(2):
+            side[f * strip : (f + 1) * strip] = cache[f, 0, pl.ds(there, strip), :]
+
+    @pl.when(s == 1)
+    def _():
+        for f in range(2):
+            side[f * strip : (f + 1) * strip] = latent[f, 0, pl.ds(there, strip), :]
+
+    for y in range(last + 1):
+        side[2 * strip + PX * y : 2 * strip + PX * (y + 1)] = fine[s, y, pl.ds(near, PX), :]
+
+
+def merge_body(w, out):
+    def step(i, _):
+        rows = pl.ds(pl.multiple_of(i * 32, 32), 32)
+        for dt in (1, 2):
+            k = [[w[dt, dy, dx, rows, :].astype(F32) for dx in range(3)] for dy in range(3)]
+            for py, a, ys in ((0, 0, (0,)), (0, 1, (1, 2)), (1, 0, (0, 1)), (1, 1, (2,))):
+                line = [functools.reduce(jnp.add, [k[y][x] for y in ys]) for x in range(3)]
+                for n, v in enumerate((line[0], line[1] + line[2], line[0] + line[1], line[2])):
+                    out[dt - 1, py, a, rows, n * 128 : (n + 1) * 128] = v.astype(BF16)
+        return 0
+
+    lax.fori_loop(0, w.shape[3] // 32, step, 0)
+
+
+def cached_body(fine, w, acc, rows_ref):
+    _, high, wide, ch = fine.shape
+    for f in range(2):
+        rows_ref[f, 0] = jnp.zeros((wide, ch), BF16)
+        rows_ref[f, high + 1] = jnp.zeros((wide, ch), BF16)
+        for y in range(high):
+            rows_ref[f, y + 1] = fine[f, y]
+    for t, taps in ((0, ((0, 0), (1, 1))), (1, ((1, 0),))):
+        lhs = lanes(
+            [
+                rows_ref[f, dy : dy + high].reshape(high * wide, ch)
+                for f, dt in taps
+                for dy in range(3)
+            ]
+        )
+        rhs = stacked(
+            [lanes([w[dt, dy, dx] for dx in range(3)]) for f, dt in taps for dy in range(3)]
+        )
+        res = dot(lhs, rhs)
+        for y in range(high):
+            acc[t, y] = edged_sum(res[y * wide : (y + 1) * wide])
+
+
+def mid_body(strip, pitch, own, side, side2, near, slant, w, w2, b, b2, out, x):
+    r, c, s, rows = places()
+    ch = own.shape[2]
+    mine = 2 - 2 * s
+    theirs = 2 * s
+    inside = jnp.where(s == 0, r > 0, r < rows - 1)
+    x[...] = jnp.zeros(x.shape, BF16)
+    for f in range(4):
+        x[f, mine + c, :strip] = own[f]
+        x[f, theirs + c, :strip] = jnp.where(inside, near[f], jnp.zeros_like(near[f]))
+        v = slant[f * strip : (f + 1) * strip]
+        x[f, theirs + 1 - c, :strip] = jnp.where(inside, v, jnp.zeros_like(v))
+    for f in range(2):
+        x[2 * s + f, mine + 1 - c, :strip] = side[f * strip : (f + 1) * strip]
+        x[2 - 2 * s + f, mine + 1 - c, :strip] = side2[f * strip : (f + 1) * strip]
+    lhs = lanes(
+        [
+            stacked([x[t + dt, dy : dy + 2].reshape(2 * pitch, ch) for t in range(2)])
+            for dt in range(3)
+            for dy in range(3)
+        ]
+    )
+    at = lax.broadcasted_iota(jnp.int32, (4 * pitch, 128), 0)
+    block = at // pitch
+    kept = at - block * pitch < strip
+    outer = jnp.where(s == 0, 0, 1)
+    kept = kept & (inside | (block % 2 != outer))
+    for ref, bias, half in ((w, b, s), (w2, b2, 1 - s)):
+        rhs = stacked(
+            [lanes([ref[dt, dy, dx] for dx in range(3)]) for dt in range(3) for dy in range(3)]
+        )
+        v = (shifted_sum(dot(lhs, rhs), 0) + bias[...]).astype(BF16).astype(F32)
+        v = v / (1.0 + jnp.exp(-v))
+        out[half] = jnp.where(kept, v, 0.0).astype(BF16)
+
+
+def halo_body(strip, acc, edge, edge2, side, side2, slant, corner2, w, out, blocks):
+    r, c, s, rows = places()
+    _, high, wide, _ = acc.shape
+    out[...] = acc[...]
+    for ref, v in ((edge, s), (edge2, 1 - s)):
+        inside = jnp.where(v == 0, r > 0, r < rows - 1)
+        dy = 2 * v
+        y = (high - 1) * v
+        k = [lanes([w[dt, dy, dx] for dx in range(3)]) for dt in range(2)]
+        first = edged_sum(dot(lanes([ref[0], ref[1]]), stacked(k)))
+        second = edged_sum(dot(ref[1], k[0]))
+        out[0, y] += jnp.where(inside, first, 0.0)
+        out[1, y] += jnp.where(inside, second, 0.0)
+    for y in range(high):
+        at = slice(2 * strip + PX * y, 2 * strip + PX * (y + 1))
+        blocks[s, y + 1] = side[at]
+        blocks[1 - s, y + 1] = side2[at]
+    for f in range(2):
+        mine = slant[4 * strip + PX * f : 4 * strip + PX * (f + 1)]
+        other = corner2[PX * f : PX * (f + 1)]
+        for v, p in ((s, mine), (1 - s, other)):
+            inside = jnp.where(v == 0, r > 0, r < rows - 1)
+            blocks[f, (high + 1) * v] = jnp.where(inside, p, jnp.zeros_like(p))
+    dx = 2 - 2 * c
+    at = lax.broadcasted_iota(jnp.int32, (PX, 128), 0)
+    x = pl.ds(pl.multiple_of((1 - c) * (wide - PX), 16), PX)
+    for t, taps in ((0, ((0, 0), (1, 1))), (1, ((1, 0),))):
+        lhs = lanes(
+            [
+                blocks[f, dy : dy + high].reshape(high * PX, blocks.shape[3])
+                for f, dt in taps
+                for dy in range(3)
+            ]
+        )
+        rhs = stacked([w[dt, dy, dx] for f, dt in taps for dy in range(3)])
+        res = dot(lhs, rhs)
+        for y in range(high):
+            p = res[y * PX : (y + 1) * PX]
+            p = jnp.where(
+                c == 1,
+                jnp.where(at == 0, pltpu.roll(p, 1, 0), 0.0),
+                jnp.where(at == PX - 1, pltpu.roll(p, PX - 1, 0), 0.0),
+            )
+            out[t, y, x, :] += p
+
+
+def final_body(strip, pitch, acc, act, act2, w, b, out, x, up):
+    _, c, s, _ = places()
+    _, high, wide, _ = acc.shape
+    for ref, v in ((act, s), (act2, 1 - s)):
+        for t in range(2):
+            for q in range(2):
+                n = (2 * t + q) * pitch
+                for h in range(2):
+                    x[t, 2 * v + q, :, h * 128 : (h + 1) * 128] = ref[h, n : n + pitch]
+    ch = x.shape[3]
+    for py in range(2):
+        part = [
+            lanes([x[f, py + a : py + a + 2].reshape(2 * pitch, ch) for a in range(2)])
+            for f in range(2)
+        ]
+        main = dot(stacked(part), stacked([w[1, py, a] for a in range(2)]))
+        late = dot(part[0], stacked([w[0, py, a] for a in range(2)]))
+        for t in range(2):
+            v = main[t * 2 * pitch : (t + 1) * 2 * pitch]
+            if t == 1:
+                v = v + late
+            even = pltpu.roll(v[:, :128], 1, 0) + v[:, 128:256]
+            odd = v[:, 256:384] + pltpu.roll(v[:, 384:], 2 * pitch - 1, 0)
+            for j in range(2):
+                at = slice(j * pitch, (j + 1) * pitch)
+                up[t, 2 * j + py, pl.ds(0, pitch, stride=2), :] = even[at]
+                up[t, 2 * j + py, pl.ds(1, pitch, stride=2), :] = odd[at]
+    first = pl.multiple_of(c * 2 * (strip - wide // 2), 16)
+    for t in range(2):
+        for y in range(high):
+            v = acc[t, y] + up[t, y, pl.ds(first, wide), :] + b[...]
+            out[t, y] = v.astype(BF16)
+
+
+def paired_body(mid_latent, mid_cache, mid_kernel, mid_offset, fine_cache, fine_kernel, fine_offset):
+    rows = lax.axis_size("row")
+    width, ch = mid_cache.shape[2:]
+    high, wide = fine_cache.shape[1:3]
+    strip = width // 2 + 8
+    pitch = -(-strip // 16) * 16
+    if pitch == strip:
+        pitch += 16
+    shape = jax.ShapeDtypeStruct
+
+    def at(r, c, s):
+        return (r * 2 + c) * 2 + s
+
+    def across(cross):
+        pairs = []
+        for c in range(2):
+            for r in range(1, rows):
+                a, b = at(r, c, 0), at(r - 1, 1 - c if cross else c, 1)
+                pairs += [(a, b), (b, a)]
+            pairs += [(at(0, c, 0), at(0, 1 - c, 0)), (at(rows - 1, c, 1), at(rows - 1, 1 - c, 1))]
+        return pairs
+
+    def neighbour(v, cross):
+        return lax.ppermute(v, ("row", "col", "sub"), across(cross))
+
+    def swap(v, axis):
+        return lax.ppermute(v, axis, [(0, 1), (1, 0)])
+
+    kernel2 = swap(mid_kernel, "sub")
+    offset2 = swap(mid_offset, "sub")
+    own, slant, side, edge = call(
+        functools.partial(pack_body, strip),
+        (
+            shape((4, strip, ch), BF16),
+            shape((4 * strip + 2 * PX, ch), BF16),
+            shape((2 * strip + high * PX, ch), BF16),
+            shape((2, wide, ch), BF16),
+        ),
+        (mid_cache, mid_latent, fine_cache),
+        name="pack",
+    )
+    slant = neighbour(slant, True)
+    side = swap(side, "col")
+    near = neighbour(own, False)
+    edge = neighbour(edge, False)
+    side2 = swap(side, "sub")
+    edge2 = swap(edge, "sub")
+    corner2 = swap(slant[4 * strip :], "sub")
+
+    merged = call(
+        merge_body, shape((2, 2, 2, ch, 512), BF16), (fine_kernel,), name="merge", flops=10**8
+    )
+    acc = call(
+        cached_body,
+        shape((2, high, wide, 128), F32),
+        (fine_cache, fine_kernel),
+        [pltpu.VMEM((2, high + 2, wide, ch), BF16)],
+        flops=2 * 9 * high * wide * ch * 384,
+        name="cached",
+    )
+    act = call(
+        functools.partial(mid_body, strip, pitch),
+        shape((2, 4 * pitch, 128), BF16),
+        (own, side, side2, near, slant, mid_kernel, kernel2, mid_offset[None], offset2[None]),
+        [pltpu.VMEM((4, 4, pitch, ch), BF16)],
+        flops=2 * 9 * 4 * pitch * ch * 768,
+        name="mid",
+    )
+    act2 = swap(act, "sub")
+    acc = call(
+        functools.partial(halo_body, strip),
+        shape(acc.shape, F32),
+        (acc, edge, edge2, side, side2, slant, corner2, fine_kernel),
+        [pltpu.VMEM((2, high + 2, PX, ch), BF16)],
+        flops=2 * 6 * wide * ch * 384,
+        name="halo",
+    )
+    return call(
+        functools.partial(final_body, strip, pitch),
+        shape((2, high, wide, 128), BF16),
+        (acc, act, act2, merged, fine_offset[None]),
+        [pltpu.VMEM((2, 4, pitch, ch), BF16), pltpu.VMEM((2, high, 2 * pitch, 128), F32)],
+        flops=2 * 12 * 2 * pitch * ch * 512,
+        name="final",
+    )
+
+
 def solution(mesh):
     placed = (
         P("video", ("row", "col"), None, None),
@@ -58,6 +392,19 @@
         P(None, None, None, None, "sub"),
         P("sub"),
     )
+    sizes = mesh.shape
+
+    def body(*args):
+        paired = (
+            sizes["col"] == 2
+            and sizes["sub"] == 2
+            and sizes["row"] > 1
+            and args[0].shape[1] == 1
+            and args[0].shape[2] % 16 == 0
+            and args[0].shape[3] == 256
+        )
+        return (paired_body if paired else general_body)(*args)
+
     return jax.shard_map(
         body, mesh=mesh, in_specs=placed, out_specs=P("video", "row", "col", "sub"), check_vma=False
     )

time: 74.2 us -> 41.4 us (0.56)
  waiting for transfers between devices: 30.3 us -> 5.44 us
  Pallas kernels: 0 us -> 21.6 us
  local copies, waits for them, and re-layouts: 14 us -> 4.01 us
  starting transfers between devices: 18.7 us -> 9.88 us
  matrix products: 6.53 us -> 0 us
  blocking collectives: 1.95 us -> 0 us
  other arithmetic: 1.89 us -> 0 us
    ppermute x6 -> x10, waiting for transfers between devices: 27.2 us -> 5.44 us  [the longest x7 4.61 us: swap(): return lax.ppermute(v, axis, [(0, 1), (1, 0)])]
    pallas_call x0 -> x6, Pallas kernels: none -> 21.6 us  [call(): pl.pallas_call(body, out_shape=listed if many else outs, in_specs=[vmem]...]
    conv_general_dilated x2 -> x0, matrix products: 6.53 us -> none  [conv_valid(): lax.conv_general_dilated(frames[None], kernel, (1, 1, 1), 'VALID', dimens...]
    ppermute x6 -> x10, starting transfers between devices: 15 us -> 9.88 us  [the longest x7 5.48 us: swap(): return lax.ppermute(v, axis, [(0, 1), (1, 0)])]
    all_to_all x1 -> x0, starting transfers between devices: 3.76 us -> none  [body(): lax.all_to_all(strip_out, 'col', split_axis=2, concat_axis=1, tiled=True)]
    all_to_all x1 -> x0, waiting for transfers between devices: 3.1 us -> none  [body(): lax.all_to_all(strip_out, 'col', split_axis=2, concat_axis=1, tiled=True)]
    reshape x1 -> x0, local copies, waits for them, and re-layouts: 2.72 us -> none  [double_size(): return jnp.repeat(jnp.repeat(field, 2, axis=1), 2, axis=2)]
    broadcast_in_dim x4 -> x0, local copies, waits for them, and re-layouts: 2.45 us -> none  [the longest x2 1.29 us: double_size(): return jnp.repeat(jnp.repeat(field, 2, axis=1), 2, axis=2)]
  transfers between devices with their start and end apart: 7 -> 10, of which waited for: 6 -> 3; matrix products, arithmetic and copies ran while one was open for 2% -> 2% of each run, Pallas kernels for 0% -> 44%
where the time goes in v1:
time: 41.4 us; the launch traced here: 41 us
  Pallas kernels  21.6 us (52%)
  starting transfers between devices  9.88 us (24%)
  waiting for transfers between devices  5.44 us (13%)
  local copies, waits for them, and re-layouts  4.01 us (10%)
    pallas_call x6, Pallas kernels, call(): pl.pallas_call(body, out_shape=listed if many else outs, in_specs=[vmem]...  21.6 us
    ppermute x7, starting transfers between devices, swap(): return lax.ppermute(v, axis, [(0, 1), (1, 0)])  5.48 us
    ppermute x7, waiting for transfers between devices, swap(): return lax.ppermute(v, axis, [(0, 1), (1, 0)])  4.61 us
    ppermute x3, starting transfers between devices, neighbour(): return lax.ppermute(v, ('row', 'col', 'sub'), across(cross))  4.4 us
    unnamed x20, local copies, waits for them, and re-layouts  3.29 us
    ppermute x3, waiting for transfers between devices, neighbour(): return lax.ppermute(v, ('row', 'col', 'sub'), across(cross))  0.83 us
  transfers between devices with their start and end apart: 10, of which 3 were waited for; matrix products, arithmetic and copies ran while one was open for 2% of the time, Pallas kernels for 44%

profile of v1, /device:TPU:0, one launch (start us, length us, event | category | flops | bytes accessed | tf_op | source)
XLA Modules:
  0.0 41.0 jit_solution(6024846773068967589)
XLA Ops:
  0.0 0.5 %collective-permute-start.7 = (bf16[3,3,3,256,128]{4,3,2,1,0:T(8,128)(2,1)}, bf16[3,3,3,256,128]{4,3,2,1,0:T(8,128)(2,1)S(1)}, u32[]{:S(2)}, u32[]{:S(2)}) collective-permute-start(bf16[3,3,3,256,128]{4,3,2,1,0:T(8,128)(2,1)} %w.6), channel_id=1, source_target_pairs={{0,1},{1,0},{2,3},{3,2},{4,5},{5,4},{6,7},{7,6},{8,9},{9,8},{10,11... | collective-permute-start | bytes 5308424 | tf_op jit(solution)/shard_map/ppermute | solution.py:324
  0.5 2.1 %pack.1 = (bf16[4,88,256]{2,1,0:T(8,128)(2,1)}, bf16[384,256]{1,0:T(8,128)(2,1)}, bf16[240,256]{1,0:T(8,128)(2,1)}, bf16[2,160,256]{2,1,0:T(8,128)(2,1)}) custom-call(bf16[2,1,160,256]{3,2,1,0:T(8,128)(2,1)} %cache.1, bf16[2,1,160,256]{3,2,1,0:T(8,128)(2,1)} %latent.1, bf16[2,4,160,256]{3,2,1,0:T(8,128)(2,1)} %fine.3), custom_call_target="tpu_custom_call" | custom-call | bytes 1646592 | tf_op jit(solution)/shard_map/pack/pallas_call | solution.py:66
  2.6 2.5 %collective-permute-start.2 = (bf16[240,256]{1,0:T(8,128)(2,1)}, bf16[240,256]{1,0:T(8,128)(2,1)S(1)}, u32[]{:S(2)}, u32[]{:S(2)}) collective-permute-start(bf16[240,256]{1,0:T(8,128)(2,1)} %get-tuple-element.10), channel_id=1, source_target_pairs={{0,2},{2,0},{1,3},{3,1},{4,6},{6,4},{5,7},{7,5},{8,10},{10,8},{9,1... | collective-permute-start | bytes 368648 | tf_op jit(solution)/shard_map/ppermute | solution.py:324
  5.1 0.0 collective-permute-start.4
  5.1 2.0 %collective-permute-start.6 = (bf16[4,88,256]{2,1,0:T(8,128)(2,1)}, bf16[4,88,256]{2,1,0:T(8,128)(2,1)S(1)}, u32[]{:S(2)}, u32[]{:S(2)}) collective-permute-start(bf16[4,88,256]{2,1,0:T(8,128)(2,1)} %get-tuple-element.12.own), channel_id=1, source_target_pairs={{4,1},{1,4},{8,5},{5,8},{12,9},{9,12},{0,2},{13,15},{6,3},{3,6},{1... | collective-permute-start | bytes 540680 | tf_op jit(solution)/shard_map/ppermute | solution.py:321
  7.1 3.6 %collective-permute-done.2.side = bf16[240,256]{1,0:T(8,128)(2,1)S(1)} collective-permute-done((bf16[240,256]{1,0:T(8,128)(2,1)}, bf16[240,256]{1,0:T(8,128)(2,1)S(1)}, u32[]{:S(2)}, u32[]{:S(2)}) %collective-permute-start.2) | collective-permute-done | bytes 122912 | tf_op jit(solution)/shard_map/ppermute | solution.py:324
  10.8 0.0 copy-start.4
  10.8 0.0 collective-permute-start.3
  10.8 0.5 %collective-permute-start.8 = (f32[128]{0:T(128)}, f32[128]{0:T(128)S(1)}, u32[]{:S(2)}, u32[]{:S(2)}) collective-permute-start(f32[128]{0:T(128)} %param.10), channel_id=1, source_target_pairs={{0,1},{1,0},{2,3},{3,2},{4,5},{5,4},{6,7},{7,6},{8,9},{9,8},{10,11... | collective-permute-start | bytes 1544 | tf_op jit(solution)/shard_map/ppermute | solution.py:324
  11.3 1.0 %collective-permute-done.8 = f32[128]{0:T(128)S(1)} collective-permute-done((f32[128]{0:T(128)}, f32[128]{0:T(128)S(1)}, u32[]{:S(2)}, u32[]{:S(2)}) %collective-permute-start.8) | collective-permute-done | bytes 544 | tf_op jit(solution)/shard_map/ppermute | solution.py:324
  12.3 0.0 copy-start.9
  12.3 2.4 %collective-permute-start = (bf16[2,160,256]{2,1,0:T(8,128)(2,1)}, bf16[2,160,256]{2,1,0:T(8,128)(2,1)S(1)}, u32[]{:S(2)}, u32[]{:S(2)}) collective-permute-start(bf16[2,160,256]{2,1,0:T(8,128)(2,1)} %get-tuple-element.9), channel_id=1, source_target_pairs={{4,1},{1,4},{8,5},{5,8},{12,9},{9,12},{0,2},{13,15},{6,3},{3,6},{1... | collective-permute-start | bytes 491528 | tf_op jit(solution)/shard_map/ppermute | solution.py:321
  14.6 0.8 %collective-permute-done.6.near = bf16[4,88,256]{2,1,0:T(8,128)(2,1)S(1)} collective-permute-done((bf16[4,88,256]{2,1,0:T(8,128)(2,1)}, bf16[4,88,256]{2,1,0:T(8,128)(2,1)S(1)}, u32[]{:S(2)}, u32[]{:S(2)}) %collective-permute-start.6) | collective-permute-done | bytes 180256 | tf_op jit(solution)/shard_map/ppermute | solution.py:321
  15.5 0.0 copy-start.8
  15.5 0.0 collective-permute-done.4.slant
  15.5 0.0 copy-start
  15.5 0.0 collective-permute-done.3.side2
  15.5 0.0 copy-start.5
  15.5 0.0 collective-permute-done.7.w2
  15.5 0.0 copy-start.7
  15.5 0.0 copy-done.4
  15.5 0.0 copy-done.9
  15.5 0.6 %copy-done.8 = bf16[4,88,256]{2,1,0:T(8,128)(2,1)} copy-done((bf16[4,88,256]{2,1,0:T(8,128)(2,1)}, bf16[4,88,256]{2,1,0:T(8,128)(2,1)S(1)}, u32[]{:S(2)}) %copy-start.8) | copy-done | bytes 180248
  16.1 0.1 copy-done
  16.2 0.0 copy-done.5
  16.2 0.6 %copy-done.7 = bf16[3,3,3,256,128]{4,3,2,1,0:T(8,128)(2,1)} copy-done((bf16[3,3,3,256,128]{4,3,2,1,0:T(8,128)(2,1)}, bf16[3,3,3,256,128]{4,3,2,1,0:T(8,128)(2,1)S(1)}, u32[]{:S(2)}) %copy-start.7) | copy-done | bytes 1769496
  16.9 5.2 %mid.1.act = bf16[2,384,128]{2,1,0:T(8,128)(2,1)} custom-call(bf16[4,88,256]{2,1,0:T(8,128)(2,1)} %get-tuple-element.12.own, bf16[240,256]{1,0:T(8,128)(2,1)} %copy-done.4, bf16[240,256]{1,0:T(8,128)(2,1)} %copy-done.5, bf16[4,88,256]{2,1,0:T(8,128)(2,1)} %copy-done.8, bf16[384,256]{1,0:T(8,128)(2,1)} %copy-done, bf16[3,3,3,256,128]{4,3,2,1,0:T(8,128)(2,1)} %w.6, ...), custom_call_target="tpu_custom_call" | custom-call | flops 1358954496 | bytes 4539392 | tf_op jit(solution)/shard_map/mid/pallas_call | solution.py:66
  22.0 1.5 %collective-permute-start.9 = (bf16[2,384,128]{2,1,0:T(8,128)(2,1)}, bf16[2,384,128]{2,1,0:T(8,128)(2,1)S(1)}, u32[]{:S(2)}, u32[]{:S(2)}) collective-permute-start(bf16[2,384,128]{2,1,0:T(8,128)(2,1)} %mid.1.act), channel_id=1, source_target_pairs={{0,1},{1,0},{2,3},{3,2},{4,5},{5,4},{6,7},{7,6},{8,9},{9,8},{10,11... | collective-permute-start | bytes 589832 | tf_op jit(solution)/shard_map/ppermute | solution.py:324
  23.5 0.0 collective-permute-done.edge
  23.5 0.0 copy-start.2
  23.5 0.1 collective-permute-start.1
  23.6 0.7 %slice.4 = bf16[32,256]{1,0:T(8,128)(2,1)S(1)} slice(bf16[384,256]{1,0:T(8,128)(2,1)} %copy-done), slice={[352:384], [0:256]} | slice | bytes 32768 | tf_op jit(solution)/shard_map/slice | solution.py:345
  24.3 0.4 %collective-permute-start.5 = (bf16[32,256]{1,0:T(8,128)(2,1)S(1)}, bf16[32,256]{1,0:T(8,128)(2,1)S(1)}, u32[]{:S(2)}, u32[]{:S(2)}) collective-permute-start(bf16[32,256]{1,0:T(8,128)(2,1)S(1)} %slice.4), channel_id=1, source_target_pairs={{0,1},{1,0},{2,3},{3,2},{4,5},{5,4},{6,7},{7,6},{8,9},{9,8},{10,11... | collective-permute-start | bytes 49160 | tf_op jit(solution)/shard_map/ppermute | solution.py:324
  24.8 4.2 %cached.1.acc = f32[2,4,160,128]{3,2,1,0:T(8,128)} custom-call(bf16[2,4,160,256]{3,2,1,0:T(8,128)(2,1)} %fine.3, bf16[3,3,3,256,128]{4,3,2,1,0:T(8,128)(2,1)} %w.7), custom_call_target="tpu_custom_call" | custom-call | flops 1132462080 | bytes 3080192 | tf_op jit(solution)/shard_map/cached/pallas_call | solution.py:66
  29.0 0.0 copy-done.2
  29.0 3.2 %merge.1.w = bf16[2,2,2,256,512]{4,3,2,1,0:T(8,128)(2,1)} custom-call(bf16[3,3,3,256,128]{4,3,2,1,0:T(8,128)(2,1)} %w.7), custom_call_target="tpu_custom_call" | custom-call | flops 100000000 | bytes 3866624 | tf_op jit(solution)/shard_map/merge/pallas_call | solution.py:66
  32.2 0.0 collective-permute-done.5.corner2
  32.2 0.0 copy-start.6
  32.2 0.0 collective-permute-done.1.edge2
  32.2 0.6 %copy-done.6 = bf16[32,256]{1,0:T(8,128)(2,1)} copy-done((bf16[32,256]{1,0:T(8,128)(2,1)}, bf16[32,256]{1,0:T(8,128)(2,1)S(1)}, u32[]{:S(2)}) %copy-start.6) | copy-done | bytes 16408
  32.8 0.0 copy-start.3
  32.8 0.7 %copy-done.3 = bf16[2,160,256]{2,1,0:T(8,128)(2,1)} copy-done((bf16[2,160,256]{2,1,0:T(8,128)(2,1)}, bf16[2,160,256]{2,1,0:T(8,128)(2,1)S(1)}, u32[]{:S(2)}) %copy-start.3) | copy-done | bytes 163864
  33.5 3.4 %halo.1.acc = f32[2,4,160,128]{3,2,1,0:T(8,128)} custom-call(f32[2,4,160,128]{3,2,1,0:T(8,128)} %cached.1.acc, bf16[2,160,256]{2,1,0:T(8,128)(2,1)} %copy-done.2, bf16[2,160,256]{2,1,0:T(8,128)(2,1)} %copy-done.3, bf16[240,256]{1,0:T(8,128)(2,1)} %copy-done.4, bf16[240,256]{1,0:T(8,128)(2,1)} %copy-done.5, bf16[384,256]{1,0:T(8,128)(2,1)} %copy-done, ...), custom_call_target="tpu_custom_call" | custom-call | flops 188743680 | bytes 3866624 | tf_op jit(solution)/shard_map/halo/pallas_call | solution.py:66
  36.8 0.0 collective-permute-done.9.act2
  36.9 0.0 copy-start.1
  36.9 0.7 %copy-done.1 = bf16[2,384,128]{2,1,0:T(8,128)(2,1)} copy-done((bf16[2,384,128]{2,1,0:T(8,128)(2,1)}, bf16[2,384,128]{2,1,0:T(8,128)(2,1)S(1)}, u32[]{:S(2)}) %copy-start.1) | copy-done | bytes 196632
  37.5 3.5 %final.1 = bf16[2,4,160,128]{3,2,1,0:T(8,128)(2,1)} custom-call(f32[2,4,160,128]{3,2,1,0:T(8,128)} %halo.1.acc, bf16[2,384,128]{2,1,0:T(8,128)(2,1)} %mid.1.act, bf16[2,384,128]{2,1,0:T(8,128)(2,1)} %copy-done.1, bf16[2,2,2,256,512]{4,3,2,1,0:T(8,128)(2,1)} %merge.1.w, f32[1,128]{1,0:T(1,128)} %bitcast.3), custom_call_target="tpu_custom_call" | custom-call | flops 603979776 | bytes 3473920 | tf_op jit(solution)/shard_map/final/pallas_call | solution.py:66
Async XLA Ops:
  0.0 15.5 %collective-permute-start.7 = (bf16[3,3,3,256,128]{4,3,2,1,0:T(8,128)(2,1)}, bf16[3,3,3,256,128]{4,3,2,1,0:T(8,128)(2,1)S(1)}, u32[]{:S(2)}, u32[]{:S(2)}) collective-permute-start(bf16[3,3,3,256,128]{4,3,2,1,0:T(8,128)(2,1)} %w.6), channel_id=1, source_target_pairs={{0,1},{1,0},{2,3},{3,2},{4,5},{5,4},{6,7},{7,6},{8,9},{9,8},{10,11... | collective-permute-start | bytes 5308424 | tf_op jit(solution)/shard_map/ppermute | solution.py:324
  2.6 8.1 %collective-permute-start.2 = (bf16[240,256]{1,0:T(8,128)(2,1)}, bf16[240,256]{1,0:T(8,128)(2,1)S(1)}, u32[]{:S(2)}, u32[]{:S(2)}) collective-permute-start(bf16[240,256]{1,0:T(8,128)(2,1)} %get-tuple-element.10), channel_id=1, source_target_pairs={{0,2},{2,0},{1,3},{3,1},{4,6},{6,4},{5,7},{7,5},{8,10},{10,8},{9,1... | collective-permute-start | bytes 368648 | tf_op jit(solution)/shard_map/ppermute | solution.py:324
  5.1 10.3 %collective-permute-start.4 = (bf16[384,256]{1,0:T(8,128)(2,1)}, bf16[384,256]{1,0:T(8,128)(2,1)S(1)}, u32[]{:S(2)}, u32[]{:S(2)}) collective-permute-start(bf16[384,256]{1,0:T(8,128)(2,1)} %get-tuple-element.11), channel_id=1, source_target_pairs={{4,3},{3,4},{8,7},{7,8},{12,11},{11,12},{0,2},{13,15},{6,1},{1,6},... | collective-permute-start | bytes 589832 | tf_op jit(solution)/shard_map/ppermute | solution.py:321
  5.1 10.3 %collective-permute-start.6 = (bf16[4,88,256]{2,1,0:T(8,128)(2,1)}, bf16[4,88,256]{2,1,0:T(8,128)(2,1)S(1)}, u32[]{:S(2)}, u32[]{:S(2)}) collective-permute-start(bf16[4,88,256]{2,1,0:T(8,128)(2,1)} %get-tuple-element.12.own), channel_id=1, source_target_pairs={{4,1},{1,4},{8,5},{5,8},{12,9},{9,12},{0,2},{13,15},{6,3},{3,6},{1... | collective-permute-start | bytes 540680 | tf_op jit(solution)/shard_map/ppermute | solution.py:321
  10.8 4.7 %copy-start.4 = (bf16[240,256]{1,0:T(8,128)(2,1)}, bf16[240,256]{1,0:T(8,128)(2,1)S(1)}, u32[]{:S(2)}) copy-start(bf16[240,256]{1,0:T(8,128)(2,1)S(1)} %collective-permute-done.2.side) | copy-start | bytes 368644
  10.8 4.7 %collective-permute-start.3 = (bf16[240,256]{1,0:T(8,128)(2,1)S(1)}, bf16[240,256]{1,0:T(8,128)(2,1)S(1)}, u32[]{:S(2)}, u32[]{:S(2)}) collective-permute-start(bf16[240,256]{1,0:T(8,128)(2,1)S(1)} %collective-permute-done.2.side), channel_id=1, source_target_pairs={{0,1},{1,0},{2,3},{3,2},{4,5},{5,4},{6,7},{7,6},{8,9},{9,8},{10,11... | collective-permute-start | bytes 368648 | tf_op jit(solution)/shard_map/ppermute | solution.py:324
  10.8 1.5 %collective-permute-start.8 = (f32[128]{0:T(128)}, f32[128]{0:T(128)S(1)}, u32[]{:S(2)}, u32[]{:S(2)}) collective-permute-start(f32[128]{0:T(128)} %param.10), channel_id=1, source_target_pairs={{0,1},{1,0},{2,3},{3,2},{4,5},{5,4},{6,7},{7,6},{8,9},{9,8},{10,11... | collective-permute-start | bytes 1544 | tf_op jit(solution)/shard_map/ppermute | solution.py:324
  12.3 3.3 %copy-start.9 = (f32[128]{0:T(128)}, f32[128]{0:T(128)S(1)}, u32[]{:S(2)}) copy-start(f32[128]{0:T(128)S(1)} %collective-permute-done.8) | copy-start | bytes 1540
  12.3 11.3 %collective-permute-start = (bf16[2,160,256]{2,1,0:T(8,128)(2,1)}, bf16[2,160,256]{2,1,0:T(8,128)(2,1)S(1)}, u32[]{:S(2)}, u32[]{:S(2)}) collective-permute-start(bf16[2,160,256]{2,1,0:T(8,128)(2,1)} %get-tuple-element.9), channel_id=1, source_target_pairs={{4,1},{1,4},{8,5},{5,8},{12,9},{9,12},{0,2},{13,15},{6,3},{3,6},{1... | collective-permute-start | bytes 491528 | tf_op jit(solution)/shard_map/ppermute | solution.py:321
  15.5 0.7 %copy-start.8 = (bf16[4,88,256]{2,1,0:T(8,128)(2,1)}, bf16[4,88,256]{2,1,0:T(8,128)(2,1)S(1)}, u32[]{:S(2)}) copy-start(bf16[4,88,256]{2,1,0:T(8,128)(2,1)S(1)} %collective-permute-done.6.near) | copy-start | bytes 540676
  15.5 0.7 %copy-start = (bf16[384,256]{1,0:T(8,128)(2,1)}, bf16[384,256]{1,0:T(8,128)(2,1)S(1)}, u32[]{:S(2)}) copy-start(bf16[384,256]{1,0:T(8,128)(2,1)S(1)} %collective-permute-done.4.slant) | copy-start | bytes 589828
  15.5 0.8 %copy-start.5 = (bf16[240,256]{1,0:T(8,128)(2,1)}, bf16[240,256]{1,0:T(8,128)(2,1)S(1)}, u32[]{:S(2)}) copy-start(bf16[240,256]{1,0:T(8,128)(2,1)S(1)} %collective-permute-done.3.side2) | copy-start | bytes 368644
  15.5 1.4 %copy-start.7 = (bf16[3,3,3,256,128]{4,3,2,1,0:T(8,128)(2,1)}, bf16[3,3,3,256,128]{4,3,2,1,0:T(8,128)(2,1)S(1)}, u32[]{:S(2)}) copy-start(bf16[3,3,3,256,128]{4,3,2,1,0:T(8,128)(2,1)S(1)} %collective-permute-done.7.w2) | copy-start | bytes 5308420
  22.0 14.8 %collective-permute-start.9 = (bf16[2,384,128]{2,1,0:T(8,128)(2,1)}, bf16[2,384,128]{2,1,0:T(8,128)(2,1)S(1)}, u32[]{:S(2)}, u32[]{:S(2)}) collective-permute-start(bf16[2,384,128]{2,1,0:T(8,128)(2,1)} %mid.1.act), channel_id=1, source_target_pairs={{0,1},{1,0},{2,3},{3,2},{4,5},{5,4},{6,7},{7,6},{8,9},{9,8},{10,11... | collective-permute-start | bytes 589832 | tf_op jit(solution)/shard_map/ppermute | solution.py:324
  23.5 5.5 %copy-start.2 = (bf16[2,160,256]{2,1,0:T(8,128)(2,1)}, bf16[2,160,256]{2,1,0:T(8,128)(2,1)S(1)}, u32[]{:S(2)}) copy-start(bf16[2,160,256]{2,1,0:T(8,128)(2,1)S(1)} %collective-permute-done.edge) | copy-start | bytes 491524
  23.5 8.7 %collective-permute-start.1 = (bf16[2,160,256]{2,1,0:T(8,128)(2,1)S(1)}, bf16[2,160,256]{2,1,0:T(8,128)(2,1)S(1)}, u32[]{:S(2)}, u32[]{:S(2)}) collective-permute-start(bf16[2,160,256]{2,1,0:T(8,128)(2,1)S(1)} %collective-permute-done.edge), channel_id=1, source_target_pairs={{0,1},{1,0},{2,3},{3,2},{4,5},{5,4},{6,7},{7,6},{8,9},{9,8},{10,11... | collective-permute-start | bytes 491528 | tf_op jit(solution)/shard_map/ppermute | solution.py:324
  24.3 7.9 %collective-permute-start.5 = (bf16[32,256]{1,0:T(8,128)(2,1)S(1)}, bf16[32,256]{1,0:T(8,128)(2,1)S(1)}, u32[]{:S(2)}, u32[]{:S(2)}) collective-permute-start(bf16[32,256]{1,0:T(8,128)(2,1)S(1)} %slice.4), channel_id=1, source_target_pairs={{0,1},{1,0},{2,3},{3,2},{4,5},{5,4},{6,7},{7,6},{8,9},{9,8},{10,11... | collective-permute-start | bytes 49160 | tf_op jit(solution)/shard_map/ppermute | solution.py:324
  32.2 0.6 %copy-start.6 = (bf16[32,256]{1,0:T(8,128)(2,1)}, bf16[32,256]{1,0:T(8,128)(2,1)S(1)}, u32[]{:S(2)}) copy-start(bf16[32,256]{1,0:T(8,128)(2,1)S(1)} %collective-permute-done.5.corner2) | copy-start | bytes 49156
  32.8 0.7 %copy-start.3 = (bf16[2,160,256]{2,1,0:T(8,128)(2,1)}, bf16[2,160,256]{2,1,0:T(8,128)(2,1)S(1)}, u32[]{:S(2)}) copy-start(bf16[2,160,256]{2,1,0:T(8,128)(2,1)S(1)} %collective-permute-done.1.edge2) | copy-start | bytes 491524
  36.9 0.7 %copy-start.1 = (bf16[2,384,128]{2,1,0:T(8,128)(2,1)}, bf16[2,384,128]{2,1,0:T(8,128)(2,1)S(1)}, u32[]{:S(2)}) copy-start(bf16[2,384,128]{2,1,0:T(8,128)(2,1)S(1)} %collective-permute-done.9.act2) | copy-start | bytes 589828

commit v2 on v1

--- a/solution.py
+++ b/solution.py
@@ -9,6 +9,7 @@
 
 BF16 = jnp.bfloat16
 F32 = jnp.float32
+GRANT = 12 * 2**20
 PX = 16
 
 
@@ -56,8 +57,9 @@
     return conv_valid(fine_frames, fine_kernel, fine_offset)
 
 
-def call(body, outs, args, scratch=(), flops=0, name=None):
+def call(body, outs, args, scratch=(), flops=0, name=None, space=pltpu.VMEM):
     vmem = pl.BlockSpec(memory_space=pltpu.VMEM)
+    given = pl.BlockSpec(memory_space=space)
     many = isinstance(outs, (tuple, list))
     listed = tuple(outs) if many else (outs,)
     size = sum(a.size * a.dtype.itemsize for a in args) + sum(
@@ -66,10 +68,11 @@
     return pl.pallas_call(
         body,
         out_shape=listed if many else outs,
-        in_specs=[vmem] * len(args),
+        in_specs=[given] * len(args),
         out_specs=(vmem,) * len(listed) if many else vmem,
         scratch_shapes=list(scratch),
         cost_estimate=pl.CostEstimate(flops=flops, bytes_accessed=size, transcendentals=0),
+        compiler_params=pltpu.CompilerParams(vmem_limit_bytes=GRANT),
         name=name,
     )(*args)
 
@@ -112,34 +115,44 @@
     return jnp.dot(a, b, preferred_element_type=F32)
 
 
-def pack_body(strip, cache, latent, fine, own, slant, side, edge):
+def pack_body(strip, cache, latent, fine, own, slant, side, edge, sems):
     _, c, s, _ = places()
     width = cache.shape[2]
     last = fine.shape[1] - 1
-    here = pl.multiple_of(c * (width - strip), 8)
-    there = pl.multiple_of((1 - c) * (width - strip), 8)
-    near = pl.multiple_of((1 - c) * (fine.shape[2] - PX), 16)
+    here = pl.ds(pl.multiple_of(c * (width - strip), 8), strip)
+    there = pl.ds(pl.multiple_of((1 - c) * (width - strip), 8), strip)
+    near = pl.ds(pl.multiple_of((1 - c) * (fine.shape[2] - PX), 16), PX)
     row = s * last
+    copies = []
+
+    def copy(source, target):
+        copies.append(pltpu.make_async_copy(source, target, sems.at[len(copies)]))
+
     for f in range(2):
-        own[f] = cache[f, 0, pl.ds(here, strip), :]
-        own[2 + f] = latent[f, 0, pl.ds(here, strip), :]
-        slant[f * strip : (f + 1) * strip] = cache[f, 0, pl.ds(there, strip), :]
-        slant[(2 + f) * strip : (3 + f) * strip] = latent[f, 0, pl.ds(there, strip), :]
-        slant[4 * strip + PX * f : 4 * strip + PX * (f + 1)] = fine[f, row, pl.ds(near, PX), :]
-        edge[f] = fine[f, row]
-
-    @pl.when(s == 0)
-    def _():
+        copy(cache.at[f, 0, there], slant.at[f * strip : (f + 1) * strip])
+        copy(latent.at[f, 0, there], slant.at[(2 + f) * strip : (3 + f) * strip])
+        copy(cache.at[f, 0, here], own.at[f])
+        copy(latent.at[f, 0, here], own.at[2 + f])
+        copy(fine.at[f, row, near], slant.at[4 * strip + PX * f : 4 * strip + PX * (f + 1)])
+        copy(fine.at[f, row], edge.at[f])
+    for y in range(last + 1):
+        at = 2 * strip + PX * y
+        copy(fine.at[s, y, near], side.at[at : at + PX])
+    common = len(copies)
+    for ref in (cache, latent):
         for f in range(2):
-            side[f * strip : (f + 1) * strip] = cache[f, 0, pl.ds(there, strip), :]
-
-    @pl.when(s == 1)
-    def _():
-        for f in range(2):
-            side[f * strip : (f + 1) * strip] = latent[f, 0, pl.ds(there, strip), :]
-
-    for y in range(last + 1):
-        side[2 * strip + PX * y : 2 * strip + PX * (y + 1)] = fine[s, y, pl.ds(near, PX), :]
+            copy(ref.at[f, 0, there], side.at[f * strip : (f + 1) * strip])
+
+    for step in ("start", "wait"):
+        for k in range(2):
+
+            @pl.when(s == k)
+            def _():
+                for one in copies[common + 2 * k : common + 2 * k + 2]:
+                    getattr(one, step)()
+
+        for one in copies[:common]:
+            getattr(one, step)()
 
 
 def merge_body(w, out):
@@ -179,7 +192,7 @@
             acc[t, y] = edged_sum(res[y * wide : (y + 1) * wide])
 
 
-def mid_body(strip, pitch, own, side, side2, near, slant, w, w2, b, b2, out, x):
+def mid_body(strip, pitch, own, side, side2, near, slant, w, w2, b, b2, _acc, _merged, out, x):
     r, c, s, rows = places()
     ch = own.shape[2]
     mine = 2 - 2 * s
@@ -323,8 +336,6 @@
     def swap(v, axis):
         return lax.ppermute(v, axis, [(0, 1), (1, 0)])
 
-    kernel2 = swap(mid_kernel, "sub")
-    offset2 = swap(mid_offset, "sub")
     own, slant, side, edge = call(
         functools.partial(pack_body, strip),
         (
@@ -333,20 +344,18 @@
             shape((2 * strip + high * PX, ch), BF16),
             shape((2, wide, ch), BF16),
         ),
-        (mid_cache, mid_latent, fine_cache),
+        [pltpu.with_memory_space_constraint(v, pltpu.HBM) for v in (mid_cache, mid_latent, fine_cache)],
+        [pltpu.SemaphoreType.DMA((2 * 6 + high + 4,))],
         name="pack",
+        space=pltpu.HBM,
     )
     slant = neighbour(slant, True)
     side = swap(side, "col")
     near = neighbour(own, False)
     edge = neighbour(edge, False)
-    side2 = swap(side, "sub")
-    edge2 = swap(edge, "sub")
-    corner2 = swap(slant[4 * strip :], "sub")
-
-    merged = call(
-        merge_body, shape((2, 2, 2, ch, 512), BF16), (fine_kernel,), name="merge", flops=10**8
-    )
+    sent, bias, own = lax.optimization_barrier((mid_kernel, mid_offset, own))
+    kernel2 = swap(sent, "sub")
+    offset2 = swap(bias, "sub")
     acc = call(
         cached_body,
         shape((2, high, wide, 128), F32),
@@ -355,10 +364,17 @@
         flops=2 * 9 * high * wide * ch * 384,
         name="cached",
     )
+    side, acc = lax.optimization_barrier((side, acc))
+    side2 = swap(side, "sub")
+    merged = call(
+        merge_body, shape((2, 2, 2, ch, 512), BF16), (fine_kernel,), name="merge", flops=10**8
+    )
+    edge2 = swap(edge, "sub")
+    corner2 = swap(slant[4 * strip :], "sub")
     act = call(
         functools.partial(mid_body, strip, pitch),
         shape((2, 4 * pitch, 128), BF16),
-        (own, side, side2, near, slant, mid_kernel, kernel2, mid_offset[None], offset2[None]),
+        (own, side, side2, near, slant, mid_kernel, kernel2, mid_offset[None], offset2[None], acc, merged),
         [pltpu.VMEM((4, 4, pitch, ch), BF16)],
         flops=2 * 9 * 4 * pitch * ch * 768,
         name="mid",

time: 41.4 us -> 21.4 us (0.52)
  Pallas kernels: 21.6 us -> 7.78 us
  starting transfers between devices: 9.88 us -> 7.44 us
  waiting for transfers between devices: 5.44 us -> 3.22 us
  local copies, waits for them, and re-layouts: 4.01 us -> 2.58 us
    pallas_call x6, Pallas kernels: 21.6 us -> 7.78 us  [call(): pl.pallas_call(body, out_shape=listed if many else outs, in_specs=[given]...]
    ppermute x7, waiting for transfers between devices: 4.61 us -> 1.74 us  [swap(): return lax.ppermute(v, axis, [(0, 1), (1, 0)])]
    ppermute x7, starting transfers between devices: 5.48 us -> 4.25 us  [swap(): return lax.ppermute(v, axis, [(0, 1), (1, 0)])]
    ppermute x3, starting transfers between devices: 4.4 us -> 3.19 us  [neighbour(): return lax.ppermute(v, ('row', 'col', 'sub'), across(cross))]
    slice x1, local copies, waits for them, and re-layouts: 0.72 us -> 0.01 us  [paired_body(): corner2 = swap(slant[4 * strip:], 'sub')]
    unnamed x20 -> x12, local copies, waits for them, and re-layouts: 3.29 us -> 2.58 us
    ppermute x3, waiting for transfers between devices: 0.83 us -> 1.48 us  [neighbour(): return lax.ppermute(v, ('row', 'col', 'sub'), across(cross))]
  transfers between devices with their start and end apart: 10 -> 10, of which waited for: 3 -> 4; matrix products, arithmetic and copies ran while one was open for 2% -> 0% of each run, Pallas kernels for 44% -> 23%
where the time goes in v2:
time: 21.4 us; the launch traced here: 21.1 us
  Pallas kernels  7.78 us (36%)
  starting transfers between devices  7.44 us (35%)
  waiting for transfers between devices  3.22 us (15%)
  local copies, waits for them, and re-layouts  2.58 us (12%)
    pallas_call x6, Pallas kernels, call(): pl.pallas_call(body, out_shape=listed if many else outs, in_specs=[given]...  7.78 us
    ppermute x7, starting transfers between devices, swap(): return lax.ppermute(v, axis, [(0, 1), (1, 0)])  4.25 us
    ppermute x3, starting transfers between devices, neighbour(): return lax.ppermute(v, ('row', 'col', 'sub'), across(cross))  3.19 us
    unnamed x12, local copies, waits for them, and re-layouts  2.58 us
    ppermute x7, waiting for transfers between devices, swap(): return lax.ppermute(v, axis, [(0, 1), (1, 0)])  1.74 us
    ppermute x3, waiting for transfers between devices, neighbour(): return lax.ppermute(v, ('row', 'col', 'sub'), across(cross))  1.48 us
  transfers between devices with their start and end apart: 10, of which 4 were waited for; matrix products, arithmetic and copies ran while one was open for 0% of the time, Pallas kernels for 23%

profile of v2, /device:TPU:0, one launch (start us, length us, event | category | flops | bytes accessed | tf_op | source)
XLA Modules:
  0.0 21.1 jit_solution(6409964987085829377)
XLA Ops:
  0.0 1.4 %pack.1 = (bf16[4,88,256]{2,1,0:T(8,128)(2,1)S(1)}, bf16[384,256]{1,0:T(8,128)(2,1)S(1)}, bf16[240,256]{1,0:T(8,128)(2,1)S(1)}, bf16[2,160,256]{2,1,0:T(8,128)(2,1)S(1)}) custom-call(bf16[2,1,160,256]{3,2,1,0:T(8,128)(2,1)} %cache.1, bf16[2,1,160,256]{3,2,1,0:T(8,128)(2,1)} %latent.1, bf16[2,4,160,256]{3,2,1,0:T(8,128)(2,1)} %fine.3), custom_call_target="tpu_custom_call" | custom-call | bytes 1646592 | tf_op jit(solution)/shard_map/pack/pallas_call | solution.py:68
  1.4 0.6 %collective-permute-start.7 = (bf16[3,3,3,256,128]{4,3,2,1,0:T(8,128)(2,1)}, bf16[3,3,3,256,128]{4,3,2,1,0:T(8,128)(2,1)S(1)}, u32[]{:S(2)}, u32[]{:S(2)}) collective-permute-start(bf16[3,3,3,256,128]{4,3,2,1,0:T(8,128)(2,1)} %w.7), channel_id=1, source_target_pairs={{0,1},{1,0},{2,3},{3,2},{4,5},{5,4},{6,7},{7,6},{8,9},{9,8},{10,11... | collective-permute-start | bytes 5308424 | tf_op jit(solution)/shard_map/ppermute | solution.py:337
  1.9 2.6 %collective-permute-start = (bf16[240,256]{1,0:T(8,128)(2,1)S(1)}, bf16[240,256]{1,0:T(8,128)(2,1)S(1)}, u32[]{:S(2)}, u32[]{:S(2)}) collective-permute-start(bf16[240,256]{1,0:T(8,128)(2,1)S(1)} %get-tuple-element.14), channel_id=1, source_target_pairs={{0,2},{2,0},{1,3},{3,1},{4,6},{6,4},{5,7},{7,5},{8,10},{10,8},{9,1... | collective-permute-start | bytes 368648 | tf_op jit(solution)/shard_map/ppermute | solution.py:337
  4.5 0.1 collective-permute-start.6
  4.6 1.9 %collective-permute-start.4 = (bf16[384,256]{1,0:T(8,128)(2,1)S(1)}, bf16[384,256]{1,0:T(8,128)(2,1)S(1)}, u32[]{:S(2)}, u32[]{:S(2)}) collective-permute-start(bf16[384,256]{1,0:T(8,128)(2,1)S(1)} %get-tuple-element.18), channel_id=1, source_target_pairs={{4,3},{3,4},{8,7},{7,8},{12,11},{11,12},{0,2},{13,15},{6,1},{1,6},... | collective-permute-start | bytes 589832 | tf_op jit(solution)/shard_map/ppermute | solution.py:334
  6.5 0.0 copy-start
  6.5 1.5 %copy-done = bf16[3,3,3,256,128]{4,3,2,1,0:T(8,128)(2,1)S(1)} copy-done((bf16[3,3,3,256,128]{4,3,2,1,0:T(8,128)(2,1)S(1)}, bf16[3,3,3,256,128]{4,3,2,1,0:T(8,128)(2,1)}, u32[]{:S(2)}) %copy-start) | copy-done | bytes 1769496
  8.0 0.0 copy-start.3
  8.0 1.1 %copy-done.3 = bf16[2,4,160,256]{3,2,1,0:T(8,128)(2,1)S(1)} copy-done((bf16[2,4,160,256]{3,2,1,0:T(8,128)(2,1)S(1)}, bf16[2,4,160,256]{3,2,1,0:T(8,128)(2,1)}, u32[]{:S(2)}) %copy-start.3) | copy-done | bytes 655384
  9.1 0.0 copy-start.4
  9.1 1.7 %cached.1.acc._acc = f32[2,4,160,128]{3,2,1,0:T(8,128)S(1)} custom-call(bf16[2,4,160,256]{3,2,1,0:T(8,128)(2,1)S(1)} %copy-done.3, bf16[3,3,3,256,128]{4,3,2,1,0:T(8,128)(2,1)S(1)} %copy-done), custom_call_target="tpu_custom_call" | custom-call | flops 1132462080 | bytes 3080192 | tf_op jit(solution)/shard_map/cached/pallas_call | solution.py:68
  10.8 0.0 collective-permute-done.side
  10.8 0.1 collective-permute-start.3
  10.9 0.0 copy-done.4
  10.9 0.5 %collective-permute-start.8 = (f32[128]{0:T(128)S(1)}, f32[128]{0:T(128)S(1)}, u32[]{:S(2)}, u32[]{:S(2)}) collective-permute-start(f32[128]{0:T(128)S(1)} %copy-done.4), channel_id=1, source_target_pairs={{0,1},{1,0},{2,3},{3,2},{4,5},{5,4},{6,7},{7,6},{8,9},{9,8},{10,11... | collective-permute-start | bytes 1544 | tf_op jit(solution)/shard_map/ppermute | solution.py:337
  11.4 0.8 %collective-permute-done.8 = f32[128]{0:T(128)S(1)} collective-permute-done((f32[128]{0:T(128)S(1)}, f32[128]{0:T(128)S(1)}, u32[]{:S(2)}, u32[]{:S(2)}) %collective-permute-start.8) | collective-permute-done | bytes 544 | tf_op jit(solution)/shard_map/ppermute | solution.py:337
  12.2 0.0 copy-start.2
  12.2 1.2 %collective-permute-start.1 = (bf16[2,160,256]{2,1,0:T(8,128)(2,1)S(1)}, bf16[2,160,256]{2,1,0:T(8,128)(2,1)S(1)}, u32[]{:S(2)}, u32[]{:S(2)}) collective-permute-start(bf16[2,160,256]{2,1,0:T(8,128)(2,1)S(1)} %get-tuple-element.16), channel_id=1, source_target_pairs={{4,1},{1,4},{8,5},{5,8},{12,9},{9,12},{0,2},{13,15},{6,3},{3,6},{1... | collective-permute-start | bytes 491528 | tf_op jit(solution)/shard_map/ppermute | solution.py:334
  13.3 0.4 %merge.1._merged.w = bf16[2,2,2,256,512]{4,3,2,1,0:T(8,128)(2,1)S(1)} custom-call(bf16[3,3,3,256,128]{4,3,2,1,0:T(8,128)(2,1)S(1)} %copy-done), custom_call_target="tpu_custom_call" | custom-call | flops 100000000 | bytes 3866624 | tf_op jit(solution)/shard_map/merge/pallas_call | solution.py:68
  13.8 0.0 collective-permute-done.6.near
  13.8 0.8 %collective-permute-done.4.slant = bf16[384,256]{1,0:T(8,128)(2,1)S(1)} collective-permute-done((bf16[384,256]{1,0:T(8,128)(2,1)S(1)}, bf16[384,256]{1,0:T(8,128)(2,1)S(1)}, u32[]{:S(2)}, u32[]{:S(2)}) %collective-permute-start.4) | collective-permute-done | bytes 196640 | tf_op jit(solution)/shard_map/ppermute | solution.py:334
  14.5 0.0 collective-permute-done.3.side2
  14.5 0.0 collective-permute-done.7.w2
  14.5 0.0 copy-done.2
  14.6 0.0 copy-start.1
  14.6 2.1 %mid.1.act = bf16[2,384,128]{2,1,0:T(8,128)(2,1)S(1)} custom-call(bf16[4,88,256]{2,1,0:T(8,128)(2,1)S(1)} %get-tuple-element.20.own, bf16[240,256]{1,0:T(8,128)(2,1)S(1)} %collective-permute-done.side, bf16[240,256]{1,0:T(8,128)(2,1)S(1)} %collective-permute-done.3.side2, bf16[4,88,256]{2,1,0:T(8,128)(2,1)S(1)} %collective-permute-done.6.near, ...), custom_call_target="tpu_custom_call" | custom-call | flops 1358954496 | bytes 7291904 | tf_op jit(solution)/shard_map/mid/pallas_call | solution.py:68
  16.7 0.1 collective-permute-start.9
  16.8 0.7 %collective-permute-done.1.edge = bf16[2,160,256]{2,1,0:T(8,128)(2,1)S(1)} collective-permute-done((bf16[2,160,256]{2,1,0:T(8,128)(2,1)S(1)}, bf16[2,160,256]{2,1,0:T(8,128)(2,1)S(1)}, u32[]{:S(2)}, u32[]{:S(2)}) %collective-permute-start.1) | collective-permute-done | bytes 163872 | tf_op jit(solution)/shard_map/ppermute | solution.py:334
  17.5 0.1 collective-permute-start.2
  17.6 0.0 copy-start.5
  17.6 0.5 %collective-permute-start.5 = (bf16[32,256]{1,0:T(8,128)(2,1)S(1)}, bf16[32,256]{1,0:T(8,128)(2,1)S(1)}, u32[]{:S(2)}, u32[]{:S(2)}) collective-permute-start(bf16[32,256]{1,0:T(8,128)(2,1)S(1)} %slice.4), channel_id=1, source_target_pairs={{0,1},{1,0},{2,3},{3,2},{4,5},{5,4},{6,7},{7,6},{8,9},{9,8},{10,11... | collective-permute-start | bytes 49160 | tf_op jit(solution)/shard_map/ppermute | solution.py:337
  18.0 0.9 %collective-permute-done.5.corner2 = bf16[32,256]{1,0:T(8,128)(2,1)S(1)} collective-permute-done((bf16[32,256]{1,0:T(8,128)(2,1)S(1)}, bf16[32,256]{1,0:T(8,128)(2,1)S(1)}, u32[]{:S(2)}, u32[]{:S(2)}) %collective-permute-start.5) | collective-permute-done | bytes 16416 | tf_op jit(solution)/shard_map/ppermute | solution.py:337
  18.9 0.0 collective-permute-done.2.edge2
  18.9 0.0 copy-done.1
  18.9 0.5 %halo.1.acc = f32[2,4,160,128]{3,2,1,0:T(8,128)S(1)} custom-call(f32[2,4,160,128]{3,2,1,0:T(8,128)S(1)} %cached.1.acc._acc, bf16[2,160,256]{2,1,0:T(8,128)(2,1)S(1)} %collective-permute-done.1.edge, bf16[2,160,256]{2,1,0:T(8,128)(2,1)S(1)} %collective-permute-done.2.edge2, bf16[240,256]{1,0:T(8,128)(2,1)S(1)} %collective-permute-done.side, ...), custom_call_target="tpu_custom_call" | custom-call | flops 188743680 | bytes 3866624 | tf_op jit(solution)/shard_map/halo/pallas_call | solution.py:68
  19.5 0.0 collective-permute-done.9.act2
  19.5 0.0 copy-done.5
  19.5 1.7 %final.1 = bf16[2,4,160,128]{3,2,1,0:T(8,128)(2,1)} custom-call(f32[2,4,160,128]{3,2,1,0:T(8,128)S(1)} %halo.1.acc, bf16[2,384,128]{2,1,0:T(8,128)(2,1)S(1)} %mid.1.act, bf16[2,384,128]{2,1,0:T(8,128)(2,1)S(1)} %collective-permute-done.9.act2, bf16[2,2,2,256,512]{4,3,2,1,0:T(8,128)(2,1)S(1)} %merge.1._merged.w, f32[1,128]{1,0:T(1,128)S(1)} %bitcast.4), custom_call_target="tpu_custom_call" | custom-call | flops 603979776 | bytes 3473920 | tf_op jit(solution)/shard_map/final/pallas_call | solution.py:68
  (1 shorter events, 0.0 us)
Async XLA Ops:
  1.4 13.2 %collective-permute-start.7 = (bf16[3,3,3,256,128]{4,3,2,1,0:T(8,128)(2,1)}, bf16[3,3,3,256,128]{4,3,2,1,0:T(8,128)(2,1)S(1)}, u32[]{:S(2)}, u32[]{:S(2)}) collective-permute-start(bf16[3,3,3,256,128]{4,3,2,1,0:T(8,128)(2,1)} %w.7), channel_id=1, source_target_pairs={{0,1},{1,0},{2,3},{3,2},{4,5},{5,4},{6,7},{7,6},{8,9},{9,8},{10,11... | collective-permute-start | bytes 5308424 | tf_op jit(solution)/shard_map/ppermute | solution.py:337
  1.9 8.8 %collective-permute-start = (bf16[240,256]{1,0:T(8,128)(2,1)S(1)}, bf16[240,256]{1,0:T(8,128)(2,1)S(1)}, u32[]{:S(2)}, u32[]{:S(2)}) collective-permute-start(bf16[240,256]{1,0:T(8,128)(2,1)S(1)} %get-tuple-element.14), channel_id=1, source_target_pairs={{0,2},{2,0},{1,3},{3,1},{4,6},{6,4},{5,7},{7,5},{8,10},{10,8},{9,1... | collective-permute-start | bytes 368648 | tf_op jit(solution)/shard_map/ppermute | solution.py:337
  4.5 9.3 %collective-permute-start.6 = (bf16[4,88,256]{2,1,0:T(8,128)(2,1)S(1)}, bf16[4,88,256]{2,1,0:T(8,128)(2,1)S(1)}, u32[]{:S(2)}, u32[]{:S(2)}) collective-permute-start(bf16[4,88,256]{2,1,0:T(8,128)(2,1)S(1)} %get-tuple-element.20.own), channel_id=1, source_target_pairs={{4,1},{1,4},{8,5},{5,8},{12,9},{9,12},{0,2},{13,15},{6,3},{3,6},{1... | collective-permute-start | bytes 540680 | tf_op jit(solution)/shard_map/ppermute | solution.py:334
  4.6 10.0 %collective-permute-start.4 = (bf16[384,256]{1,0:T(8,128)(2,1)S(1)}, bf16[384,256]{1,0:T(8,128)(2,1)S(1)}, u32[]{:S(2)}, u32[]{:S(2)}) collective-permute-start(bf16[384,256]{1,0:T(8,128)(2,1)S(1)} %get-tuple-element.18), channel_id=1, source_target_pairs={{4,3},{3,4},{8,7},{7,8},{12,11},{11,12},{0,2},{13,15},{6,1},{1,6},... | collective-permute-start | bytes 589832 | tf_op jit(solution)/shard_map/ppermute | solution.py:334
  6.5 1.5 %copy-start = (bf16[3,3,3,256,128]{4,3,2,1,0:T(8,128)(2,1)S(1)}, bf16[3,3,3,256,128]{4,3,2,1,0:T(8,128)(2,1)}, u32[]{:S(2)}) copy-start(bf16[3,3,3,256,128]{4,3,2,1,0:T(8,128)(2,1)} %w.6) | copy-start | bytes 5308420
  8.0 1.1 %copy-start.3 = (bf16[2,4,160,256]{3,2,1,0:T(8,128)(2,1)S(1)}, bf16[2,4,160,256]{3,2,1,0:T(8,128)(2,1)}, u32[]{:S(2)}) copy-start(bf16[2,4,160,256]{3,2,1,0:T(8,128)(2,1)} %fine.3) | copy-start | bytes 1966084
  9.1 1.8 %copy-start.4 = (f32[128]{0:T(128)S(1)}, f32[128]{0:T(128)}, u32[]{:S(2)}) copy-start(f32[128]{0:T(128)} %param.10) | copy-start | bytes 1540
  10.8 3.8 %collective-permute-start.3 = (bf16[240,256]{1,0:T(8,128)(2,1)S(1)}, bf16[240,256]{1,0:T(8,128)(2,1)S(1)}, u32[]{:S(2)}, u32[]{:S(2)}) collective-permute-start(bf16[240,256]{1,0:T(8,128)(2,1)S(1)} %collective-permute-done.side), channel_id=1, source_target_pairs={{0,1},{1,0},{2,3},{3,2},{4,5},{5,4},{6,7},{7,6},{8,9},{9,8},{10,11... | collective-permute-start | bytes 368648 | tf_op jit(solution)/shard_map/ppermute | solution.py:337
  10.9 1.3 %collective-permute-start.8 = (f32[128]{0:T(128)S(1)}, f32[128]{0:T(128)S(1)}, u32[]{:S(2)}, u32[]{:S(2)}) collective-permute-start(f32[128]{0:T(128)S(1)} %copy-done.4), channel_id=1, source_target_pairs={{0,1},{1,0},{2,3},{3,2},{4,5},{5,4},{6,7},{7,6},{8,9},{9,8},{10,11... | collective-permute-start | bytes 1544 | tf_op jit(solution)/shard_map/ppermute | solution.py:337
  12.2 2.4 %copy-start.2 = (bf16[3,3,3,256,128]{4,3,2,1,0:T(8,128)(2,1)S(1)}, bf16[3,3,3,256,128]{4,3,2,1,0:T(8,128)(2,1)}, u32[]{:S(2)}) copy-start(bf16[3,3,3,256,128]{4,3,2,1,0:T(8,128)(2,1)} %w.7) | copy-start | bytes 5308420
  12.2 5.3 %collective-permute-start.1 = (bf16[2,160,256]{2,1,0:T(8,128)(2,1)S(1)}, bf16[2,160,256]{2,1,0:T(8,128)(2,1)S(1)}, u32[]{:S(2)}, u32[]{:S(2)}) collective-permute-start(bf16[2,160,256]{2,1,0:T(8,128)(2,1)S(1)} %get-tuple-element.16), channel_id=1, source_target_pairs={{4,1},{1,4},{8,5},{5,8},{12,9},{9,12},{0,2},{13,15},{6,3},{3,6},{1... | collective-permute-start | bytes 491528 | tf_op jit(solution)/shard_map/ppermute | solution.py:334
  14.6 4.4 %copy-start.1 = (bf16[3,3,3,256,128]{4,3,2,1,0:T(8,128)(2,1)S(1)}, bf16[3,3,3,256,128]{4,3,2,1,0:T(8,128)(2,1)}, u32[]{:S(2)}) copy-start(bf16[3,3,3,256,128]{4,3,2,1,0:T(8,128)(2,1)} %w.6) | copy-start | bytes 5308420
  16.7 2.7 %collective-permute-start.9 = (bf16[2,384,128]{2,1,0:T(8,128)(2,1)S(1)}, bf16[2,384,128]{2,1,0:T(8,128)(2,1)S(1)}, u32[]{:S(2)}, u32[]{:S(2)}) collective-permute-start(bf16[2,384,128]{2,1,0:T(8,128)(2,1)S(1)} %mid.1.act), channel_id=1, source_target_pairs={{0,1},{1,0},{2,3},{3,2},{4,5},{5,4},{6,7},{7,6},{8,9},{9,8},{10,11... | collective-permute-start | bytes 589832 | tf_op jit(solution)/shard_map/ppermute | solution.py:337
  17.5 1.4 %collective-permute-start.2 = (bf16[2,160,256]{2,1,0:T(8,128)(2,1)S(1)}, bf16[2,160,256]{2,1,0:T(8,128)(2,1)S(1)}, u32[]{:S(2)}, u32[]{:S(2)}) collective-permute-start(bf16[2,160,256]{2,1,0:T(8,128)(2,1)S(1)} %collective-permute-done.1.edge), channel_id=1, source_target_pairs={{0,1},{1,0},{2,3},{3,2},{4,5},{5,4},{6,7},{7,6},{8,9},{9,8},{10,11... | collective-permute-start | bytes 491528 | tf_op jit(solution)/shard_map/ppermute | solution.py:337
  17.6 1.9 %copy-start.5 = (f32[128]{0:T(128)S(1)}, f32[128]{0:T(128)}, u32[]{:S(2)}) copy-start(f32[128]{0:T(128)} %param.13) | copy-start | bytes 1540
  17.6 1.4 %collective-permute-start.5 = (bf16[32,256]{1,0:T(8,128)(2,1)S(1)}, bf16[32,256]{1,0:T(8,128)(2,1)S(1)}, u32[]{:S(2)}, u32[]{:S(2)}) collective-permute-start(bf16[32,256]{1,0:T(8,128)(2,1)S(1)} %slice.4), channel_id=1, source_target_pairs={{0,1},{1,0},{2,3},{3,2},{4,5},{5,4},{6,7},{7,6},{8,9},{9,8},{10,11... | collective-permute-start | bytes 49160 | tf_op jit(solution)/shard_map/ppermute | solution.py:337
